TPU v7x, 256 devices: a whole 4x4x8 slice. The times are simulated.
256 devices in a mesh: chan: 32 (over y, x, core), tile: 8 (over z).
Axes of the slice: x: 4, y: 4, z: 8, core: 2. Of those that a mesh axis runs over, the one named last changes fastest.
Arguments:
- generator: bfloat16 [128, 1024, 1024], P('chan', 'tile'), as said below
- hamiltonian: bfloat16 [128, 1024, 1024], P('chan', 'tile')
- chan_sizes: int32 [128], P('chan'), may hold values from 512 to 1024
- pair_occupation: int32 [2, 128, 1024], P(None, 'chan'), may hold values 0 or 1
- recoupled_occupation: int32 [2, 512, 512], P(None, ('chan', 'tile')), may hold values 0 or 1
- recouple_map: int32 [512, 512], P(('chan', 'tile')), may hold values from 0 to 511, each once within a row
- recouple_weights: float32 [512, 512, 512], P(('chan', 'tile')), may hold values from -2 to 2
Outputs:
- commutator: bfloat16 [128, 1024, 1024], P('chan', 'tile')
Inputs may be any that keep to these rules, and one draw needn't show every extreme that they name: generator[c] is antisymmetric and hamiltonian[c] is symmetric in every channel.
All inputs are finite; a program needn't handle non-finite values. No bound on the sum of `pair_occupation` or of `recoupled_occupation` on one device may be relied on, other than what follows from the above.
Results may differ from a plain program's by a relative error of at most 0.0045.
Values may be sent and summed in bfloat16 or wider, within the bound.
A program may use at most 128 MiB of HBM per device.

v0:
```python
import jax
import jax.numpy as jnp
from jax import lax
from jax.sharding import PartitionSpec as P


def per_device(
    generator,
    hamiltonian,
    chan_sizes,
    pair_occupation,
    recoupled_occupation,
    recouple_map,
    recouple_weights,
):
    chan_count, tile_rows, states = generator.shape
    tile_place = lax.axis_index("tile")
    columns = lax.broadcasted_iota(jnp.int32, (chan_count, states), 1)
    live_columns = columns < chan_sizes[:, None]
    row_index = tile_place * tile_rows + lax.broadcasted_iota(jnp.int32, (chan_count, tile_rows), 1)
    live_rows = row_index < chan_sizes[:, None]
    live_mask = live_rows[:, :, None] & live_columns[:, None, :]
    zero = jnp.zeros((), jnp.bfloat16)
    eta_live = jnp.where(live_mask, generator, zero)
    gamma_live = jnp.where(live_mask, hamiltonian, zero)
    weight = (
        (1 - pair_occupation[0] - pair_occupation[1]) * live_columns.astype(jnp.int32)
    ).astype(jnp.bfloat16)
    eta_weighted = eta_live * weight[:, None, :]

    def add_rows(left, piece):
        return jnp.einsum("crk,ckj->crj", left, piece, preferred_element_type=jnp.float32)

    gamma_weighted = gamma_live * weight[:, None, :]
    first = add_rows(eta_weighted, lax.all_gather(gamma_live, "tile", axis=1, tiled=True))
    second = add_rows(gamma_weighted, lax.all_gather(eta_live, "tile", axis=1, tiled=True))
    ladder = first - second
    block_rows = chan_count * tile_rows
    ph_count, ph_states = recouple_map.shape
    flat_eta = eta_live.reshape(block_rows, states)
    flat_gamma = gamma_live.reshape(block_rows, states)
    recv_eta, recv_gamma = (
        lax.all_to_all(flat_eta, "chan", split_axis=0, concat_axis=0, tiled=True),
        lax.all_to_all(flat_gamma, "chan", split_axis=0, concat_axis=0, tiled=True),
    )
    recv_eta = recv_eta.reshape(block_rows, ph_count, ph_states)
    recv_gamma = recv_gamma.reshape(block_rows, ph_count, ph_states)
    weights_turned = jnp.transpose(recouple_weights, (1, 0, 2))
    index_map = recouple_map[None, :, :]
    eta_bar = (
        jnp.take_along_axis(recv_eta, index_map, axis=2).astype(jnp.float32) * weights_turned
    ).astype(jnp.bfloat16)
    gamma_bar = (
        jnp.take_along_axis(recv_gamma, index_map, axis=2).astype(jnp.float32) * weights_turned
    ).astype(jnp.bfloat16)
    signs = (recoupled_occupation[0] - recoupled_occupation[1]).astype(jnp.bfloat16)
    crossed = jnp.einsum(
        "iqk,kqj->iqj", eta_bar * signs[None, :, :], gamma_bar, preferred_element_type=jnp.float32
    )
    crossed = crossed - jnp.einsum(
        "iqk,kqj->iqj", gamma_bar * signs[None, :, :], eta_bar, preferred_element_type=jnp.float32
    )
    inverse = jnp.argsort(recouple_map, axis=1)
    back_bar = jnp.take_along_axis(crossed * weights_turned, inverse[None, :, :], axis=2).astype(
        jnp.bfloat16
    )
    back = lax.all_to_all(
        back_bar.reshape(block_rows, states), "chan", split_axis=0, concat_axis=0, tiled=True
    )
    total = ladder + back.reshape(chan_count, tile_rows, states).astype(jnp.float32)
    return jnp.where(live_mask, total, jnp.zeros((), jnp.float32)).astype(jnp.bfloat16)


def solution(mesh):
    return jax.shard_map(
        per_device,
        mesh=mesh,
        in_specs=(
            P("chan", "tile", None),
            P("chan", "tile", None),
            P("chan"),
            P(None, "chan", None),
            P(None, ("chan", "tile"), None),
            P(("chan", "tile"), None),
            P(("chan", "tile"), None, None),
        ),
        out_specs=P("chan", "tile", None),
        check_vma=False,
    )
```

profile of v0, /device:TPU:8, one launch (start us, length us, event | category | flops | bytes accessed | tf_op | source)
XLA Modules:
  0.0 218.8 jit_solution(13376246702962377420)
XLA Ops:
  7.4 0.0 sort.19.cloned.1.call-start
  7.4 0.6 iota.25
  8.0 0.1 sort.19.cloned.1.call-update
  8.1 0.0 all-gather.3.cloned.1.call-start
  8.1 0.7 iota_compare_fusion
  8.9 0.7 broadcast_compare_fusion
  9.6 3.4 %and_select_fusion.1 = (bf16[4,128,1024]{2,1,0:T(8,128)(2,1)}, bf16[4,128,1024]{2,1,0:T(8,128)(2,1)}) fusion(bf16[4,128,1024]{2,1,0:T(8,128)(2,1)} %param.10, pred[4,1024]{1,0:T(4,128)(4,1)S(1)} %iota_compare_fusion, pred[4,128]{1,0:T(4,128)(4,1)S(1)} %broadcast_compare_fusion, bf16[4,128,1024]{2,1,0:T(8,128)(2,1)} %param.9), kind=kLoop, calls=%fused_computation.4 | loop fusion | flops 1572864 | bytes 4198912 | tf_op jit(solution)/shard_map/jit(_where)/select_n | solution.py:25
  13.0 0.0 all-gather.3.cloned.1.call-update
  13.0 0.0 all-gather.5.cloned.1.call-start
  13.1 0.5 all-gather.5.cloned.1.call-update
  13.6 0.6 copy-done.1
  14.2 22.2 %all_to_all.24 = bf16[32,16,1024]{2,1,0:T(8,128)(2,1)S(1)} all-to-all(bf16[32,16,1024]{2,1,0:T(8,128)(2,1)S(1)} %bitcast.76), channel_id=1, replica_groups=mesh['chan'=32,'tile'=8] {'chan'}, dimensions={0} | all-to-all | bytes 2097152 | tf_op jit(solution)/shard_map/all_to_all | solution.py:43
  36.5 6.3 %all-to-all-start = ((bf16[32,16,1024]{2,1,0:T(8,128)(2,1)}), bf16[32,16,1024]{2,1,0:T(8,128)(2,1)S(1)}, u32[]{:S(2)}, u32[]{:S(2)}) async-start(bf16[32,16,1024]{2,1,0:T(8,128)(2,1)} %bitcast.3), calls=%async_computation | async-start | bytes 2097152 | tf_op jit(solution)/shard_map/all_to_all | solution.py:44
  42.8 0.0 copy-done.5
  42.8 0.0 copy-start.7
  42.8 2.9 %copy.15 = f32[2,512,512]{1,2,0:T(8,128)} copy(f32[2,512,512]{2,1,0:T(8,128)} %param.15) | data formatting | bytes 4194304 | tf_op args[6]
  45.8 0.0 copy-done.7
  45.8 0.0 sort.19.cloned.1.call-done
  45.8 0.7 fusion.20
  46.5 0.7 compare_and_fusion
  47.2 1.6 reshape.134
  48.8 2.4 %copy.16 = bf16[512,2,512]{0,2,1:T(8,128)(2,1)S(1)} copy(bf16[512,2,512]{2,1,0:T(2,128)(2,1)} %reshape.134) | data formatting | bytes 2097152 | tf_op jit(solution)/shard_map/reshape | solution.py:46
  51.3 6.3 %all-to-all-done = bf16[32,16,1024]{2,1,0:T(8,128)(2,1)S(1)} async-done(((bf16[32,16,1024]{2,1,0:T(8,128)(2,1)}), bf16[32,16,1024]{2,1,0:T(8,128)(2,1)S(1)}, u32[]{:S(2)}, u32[]{:S(2)}) %all-to-all-start) | async-done | bytes 1048608 | tf_op jit(solution)/shard_map/all_to_all | solution.py:44
  57.5 1.6 reshape.133
  59.1 2.4 %copy.14 = bf16[512,2,512]{0,2,1:T(8,128)(2,1)S(1)} copy(bf16[512,2,512]{2,1,0:T(2,128)(2,1)} %reshape.133) | data formatting | bytes 2097152 | tf_op jit(solution)/shard_map/reshape | solution.py:47
  61.6 12.3 %gather_fusion.2 = bf16[1024,512]{1,0:T(8,128)(2,1)} fusion(bf16[512,2,512]{0,2,1:T(8,128)(2,1)S(1)} %copy.16, s32[1024]{0:T(1024)S(1)} %bitcast.73), kind=kCustom, calls=%fused_computation.1.clone | custom fusion | bytes 2105344 | tf_op jit(solution)/shard_map/jit(take_along_axis)/gather | solution.py:51
  73.8 12.3 %gather_fusion.1 = bf16[1024,512]{1,0:T(8,128)(2,1)} fusion(bf16[512,2,512]{0,2,1:T(8,128)(2,1)S(1)} %copy.14, s32[1024]{0:T(1024)S(1)} %bitcast.74), kind=kCustom, calls=%fused_computation.clone | custom fusion | bytes 2105344 | tf_op jit(solution)/shard_map/jit(take_along_axis)/gather | solution.py:54
  86.1 0.0 copy-done.2
  86.1 3.7 %fusion.4 = f32[2,512,512]{2,1,0:T(8,128)S(1)} fusion(f32[2,512,512]{1,2,0:T(8,128)} %copy.15, bf16[2,512,512]{2,1,0:T(8,128)(2,1)S(1)} %bitcast.77, pred[2,512]{1,0:T(4,128)(4,1)S(1)} %and_bitcast_fusion, bf16[2,512,512]{2,1,0:T(8,128)(2,1)} %bitcast.79, bf16[2,512]{1,0:T(2,128)(2,1)S(1)} %fusion.22), kind=kOutput, calls=%fused_computation.15 | convolution fusion | flops 541589504 | bytes 6294528 | tf_op jit(solution)/shard_map/iqk,kqj->iqj/dot_general | solution.py:57
  89.8 0.0 copy-done
  89.8 0.0 copy-done.3
  89.8 0.1 copy-done.4
  90.0 1.3 bitcast_multiply_fusion
  91.3 7.3 %gather_fusion = bf16[1024,512]{1,0:T(8,128)(2,1)S(1)} fusion(bf16[512,2,512]{0,2,1:T(8,128)(2,1)S(1)} %bitcast_multiply_fusion, s32[1024]{0:T(1024)S(1)} %bitcast.75), kind=kCustom, calls=%fused_computation.2 | custom fusion | bytes 2105344 | tf_op jit(solution)/shard_map/jit(take_along_axis)/gather | solution.py:64
  98.6 1.0 copy.19
  99.6 0.8 gather.10
  100.4 0.0 copy-start.6
  100.4 0.0 copy-start.8
  100.4 1.2 select_convert_fusion
  101.6 7.1 %all-to-all-start.2 = ((bf16[32,16,1024]{2,1,0:T(8,128)(2,1)}), bf16[32,16,1024]{2,1,0:T(8,128)(2,1)}, u32[]{:S(2)}, u32[]{:S(2)}) async-start(bf16[32,16,1024]{2,1,0:T(8,128)(2,1)} %select_convert_fusion), calls=%async_computation.2 | async-start | bytes 2097152 | tf_op jit(solution)/shard_map/all_to_all | solution.py:67
  108.7 0.0 copy-done.6
  108.7 0.0 copy-done.8
  108.7 0.1 fusion.19
  108.8 1.3 all-gather.3.cloned.1.call-done
  110.1 4.6 %fusion.7 = f32[4,128,1024]{2,1,0:T(8,128)S(1)} fusion(bf16[4,1024,1024]{2,1,0:T(8,128)(2,1)} %all-gather.3.cloned.1.call-done, bf16[4,128,1024]{2,1,0:T(8,128)(2,1)S(1)} %copy-done.1, bf16[4,1024]{1,0:T(4,128)(2,1)S(1)} %fusion.19), kind=kOutput, calls=%fused_computation.18 | convolution fusion | flops 1074266112 | bytes 11542528 | tf_op jit(solution)/shard_map/crk,ckj->crj/dot_general | solution.py:32
  114.7 8.7 %all-to-all-done.2 = bf16[32,16,1024]{2,1,0:T(8,128)(2,1)} async-done(((bf16[32,16,1024]{2,1,0:T(8,128)(2,1)}), bf16[32,16,1024]{2,1,0:T(8,128)(2,1)}, u32[]{:S(2)}, u32[]{:S(2)}) %all-to-all-start.2) | async-done | bytes 1048608 | tf_op jit(solution)/shard_map/all_to_all | solution.py:67
  123.4 81.1 %all-gather.5.cloned.1.call-done = bf16[4,1024,1024]{2,1,0:T(8,128)(2,1)} async-done(((bf16[4,128,1024]{2,1,0:T(8,128)(2,1)}), bf16[4,1024,1024]{2,1,0:T(8,128)(2,1)}) %all-gather.5.cloned.1.call-update) | async-done | bytes 8388624 | tf_op jit(solution)/shard_map/all_gather | solution.py:36
  204.4 6.9 %fusion = bf16[4,128,1024]{2,1,0:T(8,128)(2,1)} fusion(bf16[4,128,1024]{2,1,0:T(8,128)(2,1)} %bitcast.20, f32[4,128,1024]{2,1,0:T(8,128)S(1)} %fusion.7, bf16[4,1024,1024]{2,1,0:T(8,128)(2,1)} %all-gather.5.cloned.1.call-done, pred[4,1024]{1,0:T(4,128)(4,1)S(1)} %iota_compare_fusion, pred[4,128]{1,0:T(4,128)(4,1)S(1)} %broadcast_compare_fusion, ...), kind=kOutput, calls=%fused_computation.6 | convolution fusion | flops 1080033280 | bytes 13644288 | tf_op jit(solution)/shard_map/crk,ckj->crj/dot_general | solution.py:32
  (13 shorter events, 0.1 us)
Async XLA Ops:
  7.4 38.4 %sort.19.cloned.1.call-start = ((), (), s32[]{:S(2)}) async-start(), calls=%async_computation.5 | async-start | bytes 24608 | tf_op jit(solution)/shard_map/jit(argsort)/sort | solution.py:63
  8.1 102.0 %all-gather.3.cloned.1.call-start = ((), (), s32[]{:S(2)}) async-start(), calls=%async_computation.3 | async-start | bytes 9437184 | tf_op jit(solution)/shard_map/all_gather | solution.py:35
  13.0 1.2 copy-start.1
  13.0 191.4 %all-gather.5.cloned.1.call-start = ((), (), s32[]{:S(2)}) async-start(), calls=%async_computation.4 | async-start | bytes 9437184 | tf_op jit(solution)/shard_map/all_gather | solution.py:36
  14.2 28.5 %copy-start.5 = (s32[2,512]{1,0:T(2,128)S(1)}, s32[2,512]{1,0:T(2,128)}, u32[]{:S(2)}) copy-start(s32[2,512]{1,0:T(2,128)} %param.14) | copy-start | bytes 12292
  36.5 21.1 %all-to-all-start = ((bf16[32,16,1024]{2,1,0:T(8,128)(2,1)}), bf16[32,16,1024]{2,1,0:T(8,128)(2,1)S(1)}, u32[]{:S(2)}, u32[]{:S(2)}) async-start(bf16[32,16,1024]{2,1,0:T(8,128)(2,1)} %bitcast.3), calls=%async_computation | async-start | bytes 2097152 | tf_op jit(solution)/shard_map/all_to_all | solution.py:44
  42.8 2.9 %copy-start.7 = (s32[2,2,512]{2,1,0:T(2,128)S(1)}, s32[2,2,512]{2,1,0:T(2,128)}, u32[]{:S(2)}) copy-start(s32[2,2,512]{2,1,0:T(2,128)} %param.13) | copy-start | bytes 24580
  73.8 12.3 %copy-start.2 = (bf16[1024,512]{1,0:T(8,128)(2,1)S(1)}, bf16[1024,512]{1,0:T(8,128)(2,1)}, u32[]{:S(2)}) copy-start(bf16[1024,512]{1,0:T(8,128)(2,1)} %gather_fusion.2) | copy-start | bytes 3145732
  86.1 3.7 %copy-start = (f32[2,512,512]{1,2,0:T(8,128)S(1)}, f32[2,512,512]{1,2,0:T(8,128)}, u32[]{:S(2)}) copy-start(f32[2,512,512]{1,2,0:T(8,128)} %copy.15) | copy-start | bytes 6291460
  86.1 3.7 %copy-start.3 = (bf16[1024,512]{1,0:T(8,128)(2,1)S(1)}, bf16[1024,512]{1,0:T(8,128)(2,1)}, u32[]{:S(2)}) copy-start(bf16[1024,512]{1,0:T(8,128)(2,1)} %gather_fusion.2) | copy-start | bytes 3145732
  86.1 3.8 %copy-start.4 = (bf16[1024,512]{1,0:T(8,128)(2,1)S(1)}, bf16[1024,512]{1,0:T(8,128)(2,1)}, u32[]{:S(2)}) copy-start(bf16[1024,512]{1,0:T(8,128)(2,1)} %gather_fusion.1) | copy-start | bytes 3145732
  100.4 8.3 %copy-start.6 = (s32[2,4,1024]{2,1,0:T(4,128)S(1)}, s32[2,4,1024]{2,1,0:T(4,128)}, u32[]{:S(2)}) copy-start(s32[2,4,1024]{2,1,0:T(4,128)} %param.12) | copy-start | bytes 98308
  100.4 8.3 %copy-start.8 = (s32[4]{0:T(128)S(1)}, s32[4]{0:T(128)}, u32[]{:S(2)}) copy-start(s32[4]{0:T(128)} %param.11) | copy-start | bytes 52
  101.6 21.8 %all-to-all-start.2 = ((bf16[32,16,1024]{2,1,0:T(8,128)(2,1)}), bf16[32,16,1024]{2,1,0:T(8,128)(2,1)}, u32[]{:S(2)}, u32[]{:S(2)}) async-start(bf16[32,16,1024]{2,1,0:T(8,128)(2,1)} %select_convert_fusion), calls=%async_computation.2 | async-start | bytes 2097152 | tf_op jit(solution)/shard_map/all_to_all | solution.py:67
Sparse Core Ops, SparseCore 0:
  10.6 3.3 sort.21.cloned.1.call-done
  (1 shorter events, 0.0 us)
Sparse Core Ops, SparseCore 1:
  13.1 96.9 all-gather.2
  111.8 92.6 all-gather.4
where the time goes:
time: 220 us; the launch traced here: 219 us
  waiting for transfers between devices  97.9 us (44%)
  local copies, waits for them, and re-layouts  46.1 us (21%)
  blocking collectives  22.2 us (10%)
  matrix products  16.5 us (8%)
  between operations  15 us (7%)
  starting transfers between devices  13.5 us (6%)
  other arithmetic  7.59 us (3%)
    all_gather x1, waiting for transfers between devices, per_device(): lax.all_gather(eta_live, 'tile', axis=1, tiled=True)  81.1 us
    all_to_all x1, blocking collectives, per_device(): lax.all_to_all(flat_eta, 'chan', split_axis=0, concat_axis=0, tiled=True)  22.2 us
    gather x1, local copies, waits for them, and re-layouts, per_device(): jnp.take_along_axis(recv_gamma, index_map, axis=2).astype(jnp.float32)  12.3 us
    gather x1, local copies, waits for them, and re-layouts, per_device(): jnp.take_along_axis(recv_eta, index_map, axis=2).astype(jnp.float32)  12.3 us
    dot_general x2, matrix products, add_rows(): jnp.einsum('crk,ckj->crj', left, piece, preferred_element_type=jnp.float32)  11.5 us
    gather x3, local copies, waits for them, and re-layouts, per_device(): jnp.take_along_axis(crossed * weights_turned, inverse[None, :, :], axis=2)  9.05 us
    all_to_all x1, waiting for transfers between devices, per_device(): lax.all_to_all(back_bar.reshape(block_rows, states), 'chan', split_axis=0...  8.65 us
    all_to_all x1, starting transfers between devices, per_device(): lax.all_to_all(back_bar.reshape(block_rows, states), 'chan', split_axis=0...  7.06 us
  transfers between devices with their start and end apart: 4, of which 4 were waited for; matrix products, arithmetic and copies ran while one was open for 26% of the time, Pallas kernels for 0%

commit v1 on v0

v1 whole, which is shorter than its diff:
```python
import functools

import jax
import jax.numpy as jnp
from jax import lax
from jax.experimental import pallas as pl
from jax.experimental.pallas import tpu as pltpu
from jax.sharding import PartitionSpec as P

MESH = pl.DeviceIdType.MESH
BF = jnp.bfloat16
F32 = jnp.float32
BLK = 128

ORDER = (0, 1, 7, 2, 6, 3, 5, 4)


def pairs_of(flip_ties):
    found = []
    for i in range(8):
        for j in range(i + 1, 8):
            a, b = ORDER[i], ORDER[j]
            if flip_ties and a + b == 8:
                a, b = b, a
            found.append((a, b))
    return found


def at128(index):
    return pl.ds(pl.multiple_of(index * BLK, BLK), BLK)


def kernel(
    n_chan,
    e_hbm,
    g_hbm,
    sizes,
    pocc,
    rocc,
    cmap,
    w_hbm,
    lad_out,
    back_out,
    e_m,
    g_m,
    rec_e,
    rec_g,
    e_full,
    g_full,
    ew,
    gw,
    lad_send,
    back_send,
    wts,
    onehot,
    e_bar,
    g_bar,
    wrow,
    load_sem,
    w_sem,
    own_sem,
    a2a_send,
    a2a_recv,
    gat_send,
    gat_recv,
    lad_ssem,
    lad_rsem,
    back_ssem,
    back_rsem,
):
    c = lax.axis_index("chan")
    t = lax.axis_index("tile")
    core = lax.rem(c, 2)
    group = 512 // n_chan

    load_e = pltpu.make_async_copy(e_hbm, e_m, load_sem.at[0])
    load_g = pltpu.make_async_copy(g_hbm, g_m, load_sem.at[1])
    load_e.start()
    load_g.start()
    load_w = pltpu.make_async_copy(w_hbm, wts, w_sem)
    load_w.start()

    barrier = pltpu.get_barrier_semaphore()

    @pl.loop(1, n_chan)
    def _(k):
        pl.semaphore_signal(barrier, inc=1, device_id=(c ^ k, t), device_id_type=MESH)

    @pl.loop(1, 8)
    def _(k):
        pl.semaphore_signal(barrier, inc=1, device_id=(c, lax.rem(t + k, 8)), device_id_type=MESH)

    cols = lax.broadcasted_iota(jnp.int32, (1, 1024), 1)
    rows = lax.broadcasted_iota(jnp.int32, (BLK, 1), 0) + t * BLK
    load_e.wait()
    load_g.wait()
    for h in range(4):
        size = sizes[h]
        col_live = (cols < size).astype(F32)
        row_live = (rows < size).astype(F32)
        wrow[h] = (1 - pocc[0, pl.ds(h, 1), :] - pocc[1, pl.ds(h, 1), :]).astype(F32) * col_live
        live = (row_live * col_live).astype(BF)
        e_m[h] = e_m[h] * live
        g_m[h] = g_m[h] * live

    pl.semaphore_wait(barrier, n_chan + 6)

    for h in range(4):
        owner = 2 * h + core
        delta = lax.rem(t - owner + 8, 8)
        far = jnp.minimum(delta, 8 - delta)

        def send(src, dst, which, j, h=h, owner=owner, delta=delta):
            pltpu.make_async_remote_copy(
                src_ref=src.at[h, :, at128(lax.rem(owner + j, 8))],
                dst_ref=dst.at[at128(delta), at128(j)],
                send_sem=gat_send,
                recv_sem=gat_recv.at[which],
                device_id=(c, owner),
                device_id_type=MESH,
            ).start()

        @pl.when(delta != 0)
        def _(send=send, far=far, delta=delta):
            send(e_m, e_full, 0, delta)
            send(g_m, g_full, 1, delta)

            @pl.when(delta < 4)
            def _():
                send(e_m, e_full, 0, 8 - delta)

            @pl.when(delta > 4)
            def _():
                send(g_m, g_full, 1, 8 - delta)

            @pl.loop(far + 1, 8 - far)
            def _(j):
                send(e_m, e_full, 0, j)
                send(g_m, g_full, 1, j)

    @pl.loop(1, n_chan)
    def _(k):
        s = c ^ k
        first = pl.multiple_of(lax.rem(s * group, BLK), group)
        mine = pl.ds(pl.multiple_of(c * group, group), group)
        for n, (src, dst) in enumerate(((e_m, rec_e), (g_m, rec_g))):
            pltpu.make_async_remote_copy(
                src_ref=src.at[(s * group) // BLK, pl.ds(first, group), :],
                dst_ref=dst.at[mine, :],
                send_sem=a2a_send,
                recv_sem=a2a_recv.at[n],
                device_id=(s, t),
                device_id_type=MESH,
            ).start()

    own_h = (c * group) // BLK
    own_rows = pl.ds(pl.multiple_of(lax.rem(c * group, BLK), group), group)
    own_place = pl.ds(pl.multiple_of(c * group, group), group)
    rec_e[own_place, :] = e_m[own_h, own_rows, :]
    rec_g[own_place, :] = g_m[own_h, own_rows, :]

    for q in range(2):
        spots = lax.broadcasted_iota(jnp.int32, (512, 512), 0)
        onehot[q] = (spots == cmap[pl.ds(q, 1), :]).astype(F32).astype(BF)

    is_owner = lax.rem(t, 2) == core

    @pl.when(is_owner)
    def _():
        h = t // 2
        for j in range(8):
            place = at128(lax.rem(t + j, 8))
            here = pl.ds(j * BLK, BLK)
            e_full[pl.ds(0, BLK), here] = e_m[h, :, place]
            g_full[pl.ds(0, BLK), here] = g_m[h, :, place]
        for n, full in enumerate((e_full, g_full)):
            landed = full.at[pl.ds(0, 28 * 16), :]
            pltpu.make_async_copy(landed, landed, gat_recv.at[n]).wait()
        for a, b in pairs_of(False):
            block = e_full[pl.ds(a * BLK, BLK), pl.ds(b * BLK, BLK)]
            e_full[pl.ds(b * BLK, BLK), pl.ds(a * BLK, BLK)] = -block.T
        for a, b in pairs_of(True):
            block = g_full[pl.ds(a * BLK, BLK), pl.ds(b * BLK, BLK)]
            g_full[pl.ds(b * BLK, BLK), pl.ds(a * BLK, BLK)] = block.T
        for j in range(8):
            here = pl.ds(j * BLK, BLK)
            weight = wrow[h, :, at128(lax.rem(t + j, 8))].astype(BF)
            ew[:, here] = e_full[:, here] * weight
            gw[:, here] = g_full[:, here] * weight

        @pl.loop(0, 4)
        def _(jj):
            half = pl.ds(pl.multiple_of(jj * 256, 256), 256)
            total = jnp.dot(ew[...], g_full[:, half], preferred_element_type=F32)
            total = total - jnp.dot(gw[...], e_full[:, half], preferred_element_type=F32)
            lad_send[:, half] = total.astype(BF)
            for i in (4, 3, 5, 2, 6, 1, 7):
                for m in range(2):
                    j = 2 * jj + m
                    pltpu.make_async_remote_copy(
                        src_ref=lad_send.at[pl.ds(i * BLK, BLK), at128(j)],
                        dst_ref=lad_out.at[h, :, at128(lax.rem(t + j, 8))],
                        send_sem=lad_ssem,
                        recv_sem=lad_rsem,
                        device_id=(c, lax.rem(t + i, 8)),
                        device_id_type=MESH,
                    ).start()
            for m in range(2):
                j = 2 * jj + m
                pltpu.make_async_copy(
                    lad_send.at[pl.ds(0, BLK), at128(j)],
                    lad_out.at[h, :, at128(lax.rem(t + j, 8))],
                    own_sem.at[0],
                ).start()

    load_w.wait()
    for n, rec in enumerate((rec_e, rec_g)):
        landed = rec.at[pl.ds(0, 512 - group), :]
        pltpu.make_async_copy(landed, landed, a2a_recv.at[n]).wait()

    @pl.loop(0, 2)
    def _(q):
        side = pl.ds(pl.multiple_of(q * 512, 512), 512)
        turn = onehot[q]
        scale = wts[q]
        e_bar[...] = (jnp.dot(rec_e[:, side], turn, preferred_element_type=F32) * scale).astype(BF)
        g_bar[...] = (jnp.dot(rec_g[:, side], turn, preferred_element_type=F32) * scale).astype(BF)
        signs = (rocc[0, pl.ds(q, 1), :] - rocc[1, pl.ds(q, 1), :]).astype(F32).astype(BF)
        crossed = jnp.dot(e_bar[...] * signs, g_bar[...], preferred_element_type=F32)
        crossed = crossed - jnp.dot(g_bar[...] * signs, e_bar[...], preferred_element_type=F32)
        scaled = (crossed * scale).astype(BF)
        back_send[:, side] = lax.dot_general(
            scaled, turn, (((1,), (1,)), ((), ())), preferred_element_type=F32
        ).astype(BF)

        @pl.loop(1, n_chan)
        def _(k):
            s = c ^ k
            pltpu.make_async_remote_copy(
                src_ref=back_send.at[pl.ds(pl.multiple_of(s * group, group), group), side],
                dst_ref=back_out.at[own_place, side],
                send_sem=back_ssem,
                recv_sem=back_rsem,
                device_id=(s, t),
                device_id_type=MESH,
            ).start()

    keep = pltpu.make_async_copy(back_send.at[own_place, :], back_out.at[own_place, :], own_sem.at[1])
    keep.start()

    def drain(ref, count, sem):
        piece = ref.at[pl.ds(0, count), :]
        pltpu.make_async_copy(piece, piece, sem).wait()

    for n in range(2):
        drain(rec_e, 512 - group, a2a_send)

    @pl.when(is_owner)
    def _():
        drain(lad_send, 20 * 16, gat_send)
        drain(lad_send, 7 * BLK, lad_ssem)
        drain(lad_send, BLK, own_sem.at[0])
        drain(lad_send, 3 * BLK, lad_rsem)

    @pl.when(jnp.logical_not(is_owner))
    def _():
        drain(lad_send, 36 * 16, gat_send)
        drain(lad_send, 4 * BLK, lad_rsem)

    keep.wait()
    drain(rec_e, 512 - group, back_ssem)
    drain(rec_e, 512 - group, back_rsem)


def exchange(n_chan, *args):
    vmem = pl.BlockSpec(memory_space=pltpu.VMEM)
    smem = pl.BlockSpec(memory_space=pltpu.SMEM)
    anywhere = pl.BlockSpec(memory_space=pl.ANY)
    dma = pltpu.SemaphoreType.DMA
    return pl.pallas_call(
        functools.partial(kernel, n_chan),
        name="commutator_exchange",
        out_shape=(
            jax.ShapeDtypeStruct((4, BLK, 1024), BF),
            jax.ShapeDtypeStruct((512, 1024), BF),
        ),
        in_specs=[anywhere, anywhere, smem, vmem, vmem, vmem, anywhere],
        out_specs=(anywhere, anywhere),
        scratch_shapes=[
            pltpu.VMEM((4, BLK, 1024), BF),
            pltpu.VMEM((4, BLK, 1024), BF),
            pltpu.VMEM((512, 1024), BF),
            pltpu.VMEM((512, 1024), BF),
            pltpu.VMEM((1024, 1024), BF),
            pltpu.VMEM((1024, 1024), BF),
            pltpu.VMEM((1024, 1024), BF),
            pltpu.VMEM((1024, 1024), BF),
            pltpu.VMEM((1024, 1024), BF),
            pltpu.VMEM((512, 1024), BF),
            pltpu.VMEM((2, 512, 512), F32),
            pltpu.VMEM((2, 512, 512), BF),
            pltpu.VMEM((512, 512), BF),
            pltpu.VMEM((512, 512), BF),
            pltpu.VMEM((4, 1, 1024), F32),
            dma((2,)),
            dma,
            dma((2,)),
            dma,
            dma((2,)),
            dma,
            dma((2,)),
            dma,
            dma,
            dma,
            dma,
        ],
        compiler_params=pltpu.CompilerParams(
            collective_id=0, has_side_effects=True, vmem_limit_bytes=56 * 1024 * 1024
        ),
    )(*args)


def per_device(
    n_chan,
    generator,
    hamiltonian,
    chan_sizes,
    pair_occupation,
    recoupled_occupation,
    recouple_map,
    recouple_weights,
):
    chan_count, tile_rows, states = generator.shape
    ladder, back = exchange(
        n_chan,
        generator,
        hamiltonian,
        chan_sizes,
        pair_occupation,
        recoupled_occupation,
        recouple_map,
        recouple_weights,
    )
    shape = (chan_count, tile_rows, states)
    sizes = chan_sizes[:, None, None]
    row = lax.axis_index("tile") * tile_rows + lax.broadcasted_iota(jnp.int32, shape, 1)
    column = lax.broadcasted_iota(jnp.int32, shape, 2)
    total = ladder.astype(F32) + back.reshape(shape).astype(F32)
    return jnp.where((row < sizes) & (column < sizes), total, jnp.zeros((), F32)).astype(BF)


def solution(mesh):
    return jax.shard_map(
        functools.partial(per_device, mesh.shape["chan"]),
        mesh=mesh,
        in_specs=(
            P("chan", "tile", None),
            P("chan", "tile", None),
            P("chan"),
            P(None, "chan", None),
            P(None, ("chan", "tile"), None),
            P(("chan", "tile"), None),
            P(("chan", "tile"), None, None),
        ),
        out_specs=P("chan", "tile", None),
        check_vma=False,
    )
```

time: 220 us -> 64.7 us (0.29)
  the two profiles are of different devices: /device:TPU:8 before, /device:TPU:1 now
where the time goes in v1:
time: 64.7 us; the launch traced here: 64.5 us
  Pallas kernels  61.4 us (95%)
  other arithmetic  3.16 us (5%)
    pallas_call x1, Pallas kernels, exchange(): pl.pallas_call(functools.partial(kernel, n_chan), name='commutator_exchan...  61.4 us
    convert_element_type x1, other arithmetic, per_device(): jnp.where((row < sizes) & (column < sizes), total, jnp.zeros((), F32))  3.16 us

profile of v1, /device:TPU:1, one launch (start us, length us, event | category | flops | bytes accessed | tf_op | source)
XLA Modules:
  0.0 64.5 jit_solution(13625773468425539644)
XLA Ops:
  0.0 0.0 copy-start
  0.0 61.4 %commutator_exchange.1 = (bf16[4,128,1024]{2,1,0:T(8,128)(2,1)}, bf16[512,1024]{1,0:T(8,128)(2,1)}) custom-call(bf16[4,128,1024]{2,1,0:T(8,128)(2,1)} %e_hbm.1, bf16[4,128,1024]{2,1,0:T(8,128)(2,1)} %g_hbm.1, s32[4]{0:T(128)} %sizes.1, s32[2,4,1024]{2,1,0:T(4,128)} %pocc.1, s32[2,2,512]{2,1,0:T(2,128)} %rocc.1, s32[2,512]{1,0:T(2,128)} %cmap.1, ...), custom_call_target="tpu_custom_call" | custom-call | tf_op jit(solution)/shard_map/commutator_exchange/pallas_call | solution.py:280
  61.4 0.0 copy-done
  61.4 3.2 %fusion.1 = bf16[4,128,1024]{2,1,0:T(8,128)(2,1)} fusion(bf16[4,128,1024]{2,1,0:T(8,128)(2,1)} %bitcast.2, bf16[4,128,1024]{2,1,0:T(8,128)(2,1)} %get-tuple-element.7, s32[4]{0:T(128)S(1)} %copy-done, s32[128]{0:T(128)S(1)} %iota_add_fusion), kind=kLoop, calls=%fused_computation.2 | loop fusion | flops 4194304 | bytes 3146256 | tf_op jit(solution)/shard_map/convert_element_type | solution.py:349
  (1 shorter events, 0.0 us)
Async XLA Ops:
  0.0 61.4 %copy-start = (s32[4]{0:T(128)S(1)}, s32[4]{0:T(128)}, u32[]{:S(2)}) copy-start(s32[4]{0:T(128)} %sizes.1) | copy-start | bytes 52

commit v2 on v1

--- a/solution.py
+++ b/solution.py
@@ -24,6 +24,29 @@
                 a, b = b, a
             found.append((a, b))
     return found
+
+
+def hops(move):
+    return min(move[0], 4 - move[0]) + min(move[1], 4 - move[1])
+
+
+def moves():
+    listed = []
+    everything = [(x, y, k) for y in range(4) for x in range(4) for k in range(2) if (x, y, k) != (0, 0, 0)]
+    for far in (1, 2, 3, 4, 0):
+        left = [m for m in everything if hops(m) == far]
+        taken = []
+        while left:
+            recent = taken[-3:][::-1]
+            cost = lambda m: sum(((m[0] == p[0]) + (m[1] == p[1])) * (3 - i) for i, p in enumerate(recent))
+            taken.append(min(left, key=cost))
+            left.remove(taken[-1])
+        listed += taken
+    return listed[::-1]
+
+
+def dot_rows(a, b):
+    return lax.dot_general(a, b, (((1,), (1,)), ((), ())), preferred_element_type=F32)
 
 
 def at128(index):
@@ -47,8 +70,7 @@
     rec_g,
     e_full,
     g_full,
-    ew,
-    gw,
+    diag,
     lad_send,
     back_send,
     wts,
@@ -73,6 +95,10 @@
     core = lax.rem(c, 2)
     group = 512 // n_chan
 
+    def target(move):
+        x, y, k = move
+        return lax.rem(c // 8 + y, 4) * 8 + lax.rem(c // 2 + x, 4) * 2 + lax.rem(core + k, 2)
+
     load_e = pltpu.make_async_copy(e_hbm, e_m, load_sem.at[0])
     load_g = pltpu.make_async_copy(g_hbm, g_m, load_sem.at[1])
     load_e.start()
@@ -105,63 +131,66 @@
 
     pl.semaphore_wait(barrier, n_chan + 6)
 
-    for h in range(4):
-        owner = 2 * h + core
-        delta = lax.rem(t - owner + 8, 8)
-        far = jnp.minimum(delta, 8 - delta)
-
-        def send(src, dst, which, j, h=h, owner=owner, delta=delta):
-            pltpu.make_async_remote_copy(
-                src_ref=src.at[h, :, at128(lax.rem(owner + j, 8))],
-                dst_ref=dst.at[at128(delta), at128(j)],
-                send_sem=gat_send,
-                recv_sem=gat_recv.at[which],
-                device_id=(c, owner),
-                device_id_type=MESH,
-            ).start()
-
-        @pl.when(delta != 0)
-        def _(send=send, far=far, delta=delta):
-            send(e_m, e_full, 0, delta)
-            send(g_m, g_full, 1, delta)
-
-            @pl.when(delta < 4)
-            def _():
-                send(e_m, e_full, 0, 8 - delta)
-
-            @pl.when(delta > 4)
-            def _():
-                send(g_m, g_full, 1, 8 - delta)
-
-            @pl.loop(far + 1, 8 - far)
-            def _(j):
-                send(e_m, e_full, 0, j)
-                send(g_m, g_full, 1, j)
-
-    @pl.loop(1, n_chan)
-    def _(k):
-        s = c ^ k
+    def gather(src, dst, which):
+        for h in range(4):
+            owner = 2 * h + core
+            delta = lax.rem(t - owner + 8, 8)
+            far = jnp.minimum(delta, 8 - delta)
+
+            def send(j, h=h, owner=owner, delta=delta):
+                pltpu.make_async_remote_copy(
+                    src_ref=src.at[h, :, at128(lax.rem(owner + j, 8))],
+                    dst_ref=dst.at[at128(delta), at128(j)],
+                    send_sem=gat_send,
+                    recv_sem=gat_recv.at[which],
+                    device_id=(c, owner),
+                    device_id_type=MESH,
+                ).start()
+
+            @pl.when(delta != 0)
+            def _(send=send, far=far, delta=delta):
+                send(delta)
+
+                @pl.when(delta > 4 if which else delta < 4)
+                def _():
+                    send(8 - delta)
+
+                @pl.loop(far + 1, 8 - far)
+                def _(j):
+                    send(j)
+
+    gather(e_m, e_full, 0)
+
+    own_place = pl.ds(pl.multiple_of(c * group, group), group)
+    for move in moves():
+        s = target(move)
         first = pl.multiple_of(lax.rem(s * group, BLK), group)
-        mine = pl.ds(pl.multiple_of(c * group, group), group)
         for n, (src, dst) in enumerate(((e_m, rec_e), (g_m, rec_g))):
             pltpu.make_async_remote_copy(
                 src_ref=src.at[(s * group) // BLK, pl.ds(first, group), :],
-                dst_ref=dst.at[mine, :],
+                dst_ref=dst.at[own_place, :],
                 send_sem=a2a_send,
                 recv_sem=a2a_recv.at[n],
                 device_id=(s, t),
                 device_id_type=MESH,
             ).start()
 
+    gather(g_m, g_full, 1)
+
     own_h = (c * group) // BLK
     own_rows = pl.ds(pl.multiple_of(lax.rem(c * group, BLK), group), group)
-    own_place = pl.ds(pl.multiple_of(c * group, group), group)
     rec_e[own_place, :] = e_m[own_h, own_rows, :]
     rec_g[own_place, :] = g_m[own_h, own_rows, :]
 
     for q in range(2):
         spots = lax.broadcasted_iota(jnp.int32, (512, 512), 0)
         onehot[q] = (spots == cmap[pl.ds(q, 1), :]).astype(F32).astype(BF)
+
+    for h in range(4):
+        weight = wrow[h].astype(BF)
+        mine = dot_rows(e_m[h] * weight, g_m[h]) + dot_rows(g_m[h] * weight, e_m[h])
+        diag[h] = mine.astype(BF)
+        pltpu.make_async_copy(diag.at[h], lad_out.at[h, :, at128(t)], own_sem.at[2]).start()
 
     is_owner = lax.rem(t, 2) == core
 
@@ -173,45 +202,52 @@
             here = pl.ds(j * BLK, BLK)
             e_full[pl.ds(0, BLK), here] = e_m[h, :, place]
             g_full[pl.ds(0, BLK), here] = g_m[h, :, place]
-        for n, full in enumerate((e_full, g_full)):
+
+        def arrive(full, which):
             landed = full.at[pl.ds(0, 28 * 16), :]
-            pltpu.make_async_copy(landed, landed, gat_recv.at[n]).wait()
-        for a, b in pairs_of(False):
-            block = e_full[pl.ds(a * BLK, BLK), pl.ds(b * BLK, BLK)]
-            e_full[pl.ds(b * BLK, BLK), pl.ds(a * BLK, BLK)] = -block.T
-        for a, b in pairs_of(True):
-            block = g_full[pl.ds(a * BLK, BLK), pl.ds(b * BLK, BLK)]
-            g_full[pl.ds(b * BLK, BLK), pl.ds(a * BLK, BLK)] = block.T
+            pltpu.make_async_copy(landed, landed, gat_recv.at[which]).wait()
+            for a, b in pairs_of(which):
+                block = full[pl.ds(a * BLK, BLK), pl.ds(b * BLK, BLK)].T
+                full[pl.ds(b * BLK, BLK), pl.ds(a * BLK, BLK)] = block if which else -block
+
+        arrive(e_full, 0)
         for j in range(8):
             here = pl.ds(j * BLK, BLK)
             weight = wrow[h, :, at128(lax.rem(t + j, 8))].astype(BF)
-            ew[:, here] = e_full[:, here] * weight
-            gw[:, here] = g_full[:, here] * weight
+            e_full[:, here] = e_full[:, here] * weight
+        arrive(g_full, 1)
 
         @pl.loop(0, 4)
         def _(jj):
             half = pl.ds(pl.multiple_of(jj * 256, 256), 256)
-            total = jnp.dot(ew[...], g_full[:, half], preferred_element_type=F32)
-            total = total - jnp.dot(gw[...], e_full[:, half], preferred_element_type=F32)
+            total = jnp.dot(e_full[...], g_full[:, half], preferred_element_type=F32)
+            total = total + dot_rows(g_full[...], e_full[half, :])
             lad_send[:, half] = total.astype(BF)
             for i in (4, 3, 5, 2, 6, 1, 7):
                 for m in range(2):
                     j = 2 * jj + m
-                    pltpu.make_async_remote_copy(
-                        src_ref=lad_send.at[pl.ds(i * BLK, BLK), at128(j)],
-                        dst_ref=lad_out.at[h, :, at128(lax.rem(t + j, 8))],
-                        send_sem=lad_ssem,
-                        recv_sem=lad_rsem,
-                        device_id=(c, lax.rem(t + i, 8)),
-                        device_id_type=MESH,
-                    ).start()
+
+                    @pl.when(j != i)
+                    def _(i=i, j=j):
+                        pltpu.make_async_remote_copy(
+                            src_ref=lad_send.at[pl.ds(i * BLK, BLK), at128(j)],
+                            dst_ref=lad_out.at[h, :, at128(lax.rem(t + j, 8))],
+                            send_sem=lad_ssem,
+                            recv_sem=lad_rsem,
+                            device_id=(c, lax.rem(t + i, 8)),
+                            device_id_type=MESH,
+                        ).start()
+
             for m in range(2):
                 j = 2 * jj + m
-                pltpu.make_async_copy(
-                    lad_send.at[pl.ds(0, BLK), at128(j)],
-                    lad_out.at[h, :, at128(lax.rem(t + j, 8))],
-                    own_sem.at[0],
-                ).start()
+
+                @pl.when(j != 0)
+                def _(j=j):
+                    pltpu.make_async_copy(
+                        lad_send.at[pl.ds(0, BLK), at128(j)],
+                        lad_out.at[h, :, at128(lax.rem(t + j, 8))],
+                        own_sem.at[0],
+                    ).start()
 
     load_w.wait()
     for n, rec in enumerate((rec_e, rec_g)):
@@ -229,13 +265,9 @@
         crossed = jnp.dot(e_bar[...] * signs, g_bar[...], preferred_element_type=F32)
         crossed = crossed - jnp.dot(g_bar[...] * signs, e_bar[...], preferred_element_type=F32)
         scaled = (crossed * scale).astype(BF)
-        back_send[:, side] = lax.dot_general(
-            scaled, turn, (((1,), (1,)), ((), ())), preferred_element_type=F32
-        ).astype(BF)
-
-        @pl.loop(1, n_chan)
-        def _(k):
-            s = c ^ k
+        back_send[:, side] = dot_rows(scaled, turn).astype(BF)
+        for move in moves():
+            s = target(move)
             pltpu.make_async_remote_copy(
                 src_ref=back_send.at[pl.ds(pl.multiple_of(s * group, group), group), side],
                 dst_ref=back_out.at[own_place, side],
@@ -258,16 +290,17 @@
     @pl.when(is_owner)
     def _():
         drain(lad_send, 20 * 16, gat_send)
-        drain(lad_send, 7 * BLK, lad_ssem)
-        drain(lad_send, BLK, own_sem.at[0])
-        drain(lad_send, 3 * BLK, lad_rsem)
+        drain(lad_send, 49 * 16, lad_ssem)
+        drain(lad_send, 7 * 16, own_sem.at[0])
+        drain(lad_send, 3 * 7 * 16, lad_rsem)
 
     @pl.when(jnp.logical_not(is_owner))
     def _():
         drain(lad_send, 36 * 16, gat_send)
-        drain(lad_send, 4 * BLK, lad_rsem)
+        drain(lad_send, 4 * 7 * 16, lad_rsem)
 
     keep.wait()
+    drain(lad_send, 4 * 16, own_sem.at[2])
     drain(rec_e, 512 - group, back_ssem)
     drain(rec_e, 512 - group, back_rsem)
 
@@ -293,8 +326,7 @@
             pltpu.VMEM((512, 1024), BF),
             pltpu.VMEM((1024, 1024), BF),
             pltpu.VMEM((1024, 1024), BF),
-            pltpu.VMEM((1024, 1024), BF),
-            pltpu.VMEM((1024, 1024), BF),
+            pltpu.VMEM((4, BLK, BLK), BF),
             pltpu.VMEM((1024, 1024), BF),
             pltpu.VMEM((512, 1024), BF),
             pltpu.VMEM((2, 512, 512), F32),
@@ -304,7 +336,7 @@
             pltpu.VMEM((4, 1, 1024), F32),
             dma((2,)),
             dma,
-            dma((2,)),
+            dma((3,)),
             dma,
             dma((2,)),
             dma,
@@ -318,6 +350,28 @@
             collective_id=0, has_side_effects=True, vmem_limit_bytes=56 * 1024 * 1024
         ),
     )(*args)
+
+
+def combine_kernel(sizes, ladder, back, out):
+    h = pl.program_id(0)
+    size = sizes[h]
+    row = lax.broadcasted_iota(jnp.int32, (BLK, 1), 0) + lax.axis_index("tile") * BLK
+    column = lax.broadcasted_iota(jnp.int32, (1, 1024), 1)
+    live = (row < size).astype(F32) * (column < size).astype(F32)
+    total = ladder[...].astype(F32) + back[...].astype(F32)
+    out[...] = jnp.where(live > 0, total, 0.0).astype(BF)
+
+
+def combine(sizes, ladder, back):
+    piece = pl.BlockSpec((None, BLK, 1024), lambda h: (h, 0, 0))
+    return pl.pallas_call(
+        combine_kernel,
+        name="combine",
+        grid=(4,),
+        out_shape=jax.ShapeDtypeStruct(ladder.shape, BF),
+        in_specs=[pl.BlockSpec(memory_space=pltpu.SMEM), piece, piece],
+        out_specs=piece,
+    )(sizes, ladder, back)
 
 
 def per_device(
@@ -341,12 +395,7 @@
         recouple_map,
         recouple_weights,
     )
-    shape = (chan_count, tile_rows, states)
-    sizes = chan_sizes[:, None, None]
-    row = lax.axis_index("tile") * tile_rows + lax.broadcasted_iota(jnp.int32, shape, 1)
-    column = lax.broadcasted_iota(jnp.int32, shape, 2)
-    total = ladder.astype(F32) + back.reshape(shape).astype(F32)
-    return jnp.where((row < sizes) & (column < sizes), total, jnp.zeros((), F32)).astype(BF)
+    return combine(chan_sizes, ladder, back.reshape(chan_count, tile_rows, states))
 
 
 def solution(mesh):

time: 64.7 us -> 59.8 us (0.924)
  other arithmetic: 3.16 us -> 0 us
  Pallas kernels: 61.4 us -> 59.6 us
    pallas_call x1, Pallas kernels: 61.4 us -> 55.8 us  [exchange(): pl.pallas_call(functools.partial(kernel, n_chan), name='commutator_exchan...]
    pallas_call x0 -> x1, Pallas kernels: none -> 3.78 us  [combine(): pl.pallas_call(combine_kernel, name='combine', grid=(4,), out_shape=jax.S...]
    convert_element_type x1 -> x0, other arithmetic: 3.16 us -> none  [per_device(): jnp.where((row < sizes) & (column < sizes), total, jnp.zeros((), F32))]
where the time goes in v2:
time: 59.8 us; the launch traced here: 59.6 us
  Pallas kernels  59.6 us (100%)
    pallas_call x1, Pallas kernels, exchange(): pl.pallas_call(functools.partial(kernel, n_chan), name='commutator_exchan...  55.8 us
    pallas_call x1, Pallas kernels, combine(): pl.pallas_call(combine_kernel, name='combine', grid=(4,), out_shape=jax.S...  3.78 us

profile of v2, /device:TPU:1, one launch (start us, length us, event | category | flops | bytes accessed | tf_op | source)
XLA Modules:
  0.0 59.6 jit_solution(11631034568685932379)
XLA Ops:
  0.0 55.8 %commutator_exchange.1 = (bf16[4,128,1024]{2,1,0:T(8,128)(2,1)}, bf16[512,1024]{1,0:T(8,128)(2,1)}) custom-call(bf16[4,128,1024]{2,1,0:T(8,128)(2,1)} %e_hbm.1, bf16[4,128,1024]{2,1,0:T(8,128)(2,1)} %g_hbm.1, s32[4]{0:T(128)} %sizes.3, s32[2,4,1024]{2,1,0:T(4,128)} %pocc.1, s32[2,2,512]{2,1,0:T(2,128)} %rocc.1, s32[2,512]{1,0:T(2,128)} %cmap.1, ...), custom_call_target="tpu_custom_call" | custom-call | tf_op jit(solution)/shard_map/commutator_exchange/pallas_call | solution.py:313
  55.8 3.8 %combine.1 = bf16[4,128,1024]{2,1,0:T(8,128)(2,1)} custom-call(s32[4]{0:T(128)} %sizes.3, bf16[4,128,1024]{2,1,0:T(8,128)(2,1)} %get-tuple-element.7.ladder, bf16[4,128,1024]{2,1,0:T(8,128)(2,1)} %bitcast.1), custom_call_target="tpu_custom_call" | custom-call | tf_op jit(solution)/shard_map/combine/pallas_call | solution.py:367

commit v3 on v2

--- a/solution.py
+++ b/solution.py
@@ -11,6 +11,7 @@
 BF = jnp.bfloat16
 F32 = jnp.float32
 BLK = 128
+VMEM_BYTES = 30 * 1024 * 1024
 
 ORDER = (0, 1, 7, 2, 6, 3, 5, 4)
 
@@ -58,9 +59,9 @@
     e_hbm,
     g_hbm,
     sizes,
-    pocc,
-    rocc,
-    cmap,
+    pocc_hbm,
+    rocc_hbm,
+    cmap_hbm,
     w_hbm,
     lad_out,
     back_out,
@@ -78,6 +79,9 @@
     e_bar,
     g_bar,
     wrow,
+    pocc,
+    rocc,
+    cmap,
     load_sem,
     w_sem,
     own_sem,
@@ -103,6 +107,12 @@
     load_g = pltpu.make_async_copy(g_hbm, g_m, load_sem.at[1])
     load_e.start()
     load_g.start()
+    small = [
+        pltpu.make_async_copy(src, dst, load_sem.at[n])
+        for n, (src, dst) in enumerate(((pocc_hbm, pocc), (cmap_hbm, cmap), (rocc_hbm, rocc)), 2)
+    ]
+    for load in small:
+        load.start()
     load_w = pltpu.make_async_copy(w_hbm, wts, w_sem)
     load_w.start()
 
@@ -120,6 +130,7 @@
     rows = lax.broadcasted_iota(jnp.int32, (BLK, 1), 0) + t * BLK
     load_e.wait()
     load_g.wait()
+    small[0].wait()
     for h in range(4):
         size = sizes[h]
         col_live = (cols < size).astype(F32)
@@ -131,9 +142,9 @@
 
     pl.semaphore_wait(barrier, n_chan + 6)
 
-    def gather(src, dst, which):
-        for h in range(4):
-            owner = 2 * h + core
+    def gather(src, dst, which, phase):
+        for h in (2 * phase, 2 * phase + 1):
+            owner = 4 * (h % 2) + phase + 2 * core
             delta = lax.rem(t - owner + 8, 8)
             far = jnp.minimum(delta, 8 - delta)
 
@@ -159,7 +170,8 @@
                 def _(j):
                     send(j)
 
-    gather(e_m, e_full, 0)
+    gather(e_m, e_full, 0, 0)
+    gather(g_m, g_full, 1, 0)
 
     own_place = pl.ds(pl.multiple_of(c * group, group), group)
     for move in moves():
@@ -175,13 +187,16 @@
                 device_id_type=MESH,
             ).start()
 
-    gather(g_m, g_full, 1)
+    gather(e_m, e_full, 0, 1)
+    gather(g_m, g_full, 1, 1)
 
     own_h = (c * group) // BLK
     own_rows = pl.ds(pl.multiple_of(lax.rem(c * group, BLK), group), group)
     rec_e[own_place, :] = e_m[own_h, own_rows, :]
     rec_g[own_place, :] = g_m[own_h, own_rows, :]
 
+    small[1].wait()
+    small[2].wait()
     for q in range(2):
         spots = lax.broadcasted_iota(jnp.int32, (512, 512), 0)
         onehot[q] = (spots == cmap[pl.ds(q, 1), :]).astype(F32).astype(BF)
@@ -192,11 +207,11 @@
         diag[h] = mine.astype(BF)
         pltpu.make_async_copy(diag.at[h], lad_out.at[h, :, at128(t)], own_sem.at[2]).start()
 
-    is_owner = lax.rem(t, 2) == core
+    is_owner = lax.rem(t // 2, 2) == core
 
     @pl.when(is_owner)
     def _():
-        h = t // 2
+        h = 2 * lax.rem(t, 2) + t // 4
         for j in range(8):
             place = at128(lax.rem(t + j, 8))
             here = pl.ds(j * BLK, BLK)
@@ -306,7 +321,7 @@
 
 
 def exchange(n_chan, *args):
-    vmem = pl.BlockSpec(memory_space=pltpu.VMEM)
+    far = pl.BlockSpec(memory_space=pltpu.HBM)
     smem = pl.BlockSpec(memory_space=pltpu.SMEM)
     anywhere = pl.BlockSpec(memory_space=pl.ANY)
     dma = pltpu.SemaphoreType.DMA
@@ -317,7 +332,7 @@
             jax.ShapeDtypeStruct((4, BLK, 1024), BF),
             jax.ShapeDtypeStruct((512, 1024), BF),
         ),
-        in_specs=[anywhere, anywhere, smem, vmem, vmem, vmem, anywhere],
+        in_specs=[far, far, smem, far, far, far, far],
         out_specs=(anywhere, anywhere),
         scratch_shapes=[
             pltpu.VMEM((4, BLK, 1024), BF),
@@ -334,7 +349,10 @@
             pltpu.VMEM((512, 512), BF),
             pltpu.VMEM((512, 512), BF),
             pltpu.VMEM((4, 1, 1024), F32),
-            dma((2,)),
+            pltpu.VMEM((2, 4, 1024), jnp.int32),
+            pltpu.VMEM((2, 2, 512), jnp.int32),
+            pltpu.VMEM((2, 512), jnp.int32),
+            dma((5,)),
             dma,
             dma((3,)),
             dma,
@@ -347,31 +365,9 @@
             dma,
         ],
         compiler_params=pltpu.CompilerParams(
-            collective_id=0, has_side_effects=True, vmem_limit_bytes=56 * 1024 * 1024
+            collective_id=0, has_side_effects=True, vmem_limit_bytes=VMEM_BYTES
         ),
-    )(*args)
-
-
-def combine_kernel(sizes, ladder, back, out):
-    h = pl.program_id(0)
-    size = sizes[h]
-    row = lax.broadcasted_iota(jnp.int32, (BLK, 1), 0) + lax.axis_index("tile") * BLK
-    column = lax.broadcasted_iota(jnp.int32, (1, 1024), 1)
-    live = (row < size).astype(F32) * (column < size).astype(F32)
-    total = ladder[...].astype(F32) + back[...].astype(F32)
-    out[...] = jnp.where(live > 0, total, 0.0).astype(BF)
-
-
-def combine(sizes, ladder, back):
-    piece = pl.BlockSpec((None, BLK, 1024), lambda h: (h, 0, 0))
-    return pl.pallas_call(
-        combine_kernel,
-        name="combine",
-        grid=(4,),
-        out_shape=jax.ShapeDtypeStruct(ladder.shape, BF),
-        in_specs=[pl.BlockSpec(memory_space=pltpu.SMEM), piece, piece],
-        out_specs=piece,
-    )(sizes, ladder, back)
+    )(*[pltpu.with_memory_space_constraint(a, pltpu.HBM) for a in args])
 
 
 def per_device(
@@ -395,7 +391,12 @@
         recouple_map,
         recouple_weights,
     )
-    return combine(chan_sizes, ladder, back.reshape(chan_count, tile_rows, states))
+    shape = (chan_count, tile_rows, states)
+    sizes = chan_sizes[:, None, None]
+    row = lax.axis_index("tile") * tile_rows + lax.broadcasted_iota(jnp.int32, shape, 1)
+    column = lax.broadcasted_iota(jnp.int32, shape, 2)
+    total = ladder.astype(F32) + back.reshape(shape).astype(F32)
+    return jnp.where((row < sizes) & (column < sizes), total, jnp.zeros((), F32)).astype(BF)
 
 
 def solution(mesh):

time: 59.8 us -> 56.3 us (0.941)
  Pallas kernels: 59.6 us -> 54.6 us
  other arithmetic: 0 us -> 1.62 us
    pallas_call x1 -> x0, Pallas kernels: 3.78 us -> none  [combine(): pl.pallas_call(combine_kernel, name='combine', grid=(4,), out_shape=jax.S...]
    convert_element_type x0 -> x1, other arithmetic: none -> 1.61 us  [per_device(): jnp.where((row < sizes) & (column < sizes), total, jnp.zeros((), F32))]
    pallas_call x1, Pallas kernels: 55.8 us -> 54.6 us  [exchange(): pl.pallas_call(functools.partial(kernel, n_chan), name='commutator_exchan...]
where the time goes in v3:
time: 56.3 us; the launch traced here: 56.2 us
  Pallas kernels  54.6 us (97%)
  other arithmetic  1.62 us (3%)
    pallas_call x1, Pallas kernels, exchange(): pl.pallas_call(functools.partial(kernel, n_chan), name='commutator_exchan...  54.6 us
    convert_element_type x1, other arithmetic, per_device(): jnp.where((row < sizes) & (column < sizes), total, jnp.zeros((), F32))  1.61 us

profile of v3, /device:TPU:1, one launch (start us, length us, event | category | flops | bytes accessed | tf_op | source)
XLA Modules:
  0.0 56.2 jit_solution(9819482435012175937)
XLA Ops:
  0.0 0.0 copy-start
  0.0 54.6 %commutator_exchange.1 = (bf16[4,128,1024]{2,1,0:T(8,128)(2,1)S(1)}, bf16[512,1024]{1,0:T(8,128)(2,1)S(1)}) custom-call(bf16[4,128,1024]{2,1,0:T(8,128)(2,1)} %e_hbm.1, bf16[4,128,1024]{2,1,0:T(8,128)(2,1)} %g_hbm.1, s32[4]{0:T(128)} %sizes.1, s32[2,4,1024]{2,1,0:T(4,128)} %pocc_hbm.1, s32[2,2,512]{2,1,0:T(2,128)} %rocc_hbm.1, s32[2,512]{1,0:T(2,128)} %cmap_hbm.1, ...), custom_call_target="tpu_custom_call" | custom-call | tf_op jit(solution)/shard_map/commutator_exchange/pallas_call | solution.py:328
  54.6 0.0 copy-done
  54.6 1.6 %fusion.1 = bf16[4,128,1024]{2,1,0:T(8,128)(2,1)} fusion(bf16[4,128,1024]{2,1,0:T(8,128)(2,1)S(1)} %bitcast.2, bf16[4,128,1024]{2,1,0:T(8,128)(2,1)S(1)} %get-tuple-element.7, s32[4]{0:T(128)S(1)} %copy-done, s32[128]{0:T(128)S(1)} %iota_add_fusion), kind=kLoop, calls=%fused_computation.2 | loop fusion | flops 4194304 | bytes 3146256 | tf_op jit(solution)/shard_map/convert_element_type | solution.py:399
  (1 shorter events, 0.0 us)
Async XLA Ops:
  0.0 54.6 %copy-start = (s32[4]{0:T(128)S(1)}, s32[4]{0:T(128)}, u32[]{:S(2)}) copy-start(s32[4]{0:T(128)} %sizes.1) | copy-start | bytes 52

commit v4 on v3

--- a/solution.py
+++ b/solution.py
@@ -82,6 +82,8 @@
     pocc,
     rocc,
     cmap,
+    held,
+    turned,
     load_sem,
     w_sem,
     own_sem,
@@ -93,6 +95,9 @@
     lad_rsem,
     back_ssem,
     back_rsem,
+    held_rsem,
+    pass_ssem,
+    pass_own,
 ):
     c = lax.axis_index("chan")
     t = lax.axis_index("tile")
@@ -171,23 +176,27 @@
                     send(j)
 
     gather(e_m, e_full, 0, 0)
+    gather(e_m, e_full, 0, 1)
     gather(g_m, g_full, 1, 0)
 
     own_place = pl.ds(pl.multiple_of(c * group, group), group)
-    for move in moves():
-        s = target(move)
-        first = pl.multiple_of(lax.rem(s * group, BLK), group)
-        for n, (src, dst) in enumerate(((e_m, rec_e), (g_m, rec_g))):
-            pltpu.make_async_remote_copy(
-                src_ref=src.at[(s * group) // BLK, pl.ds(first, group), :],
-                dst_ref=dst.at[own_place, :],
-                send_sem=a2a_send,
-                recv_sem=a2a_recv.at[n],
-                device_id=(s, t),
-                device_id_type=MESH,
-            ).start()
-
-    gather(e_m, e_full, 0, 1)
+
+    @pl.loop(0, 2)
+    def _(q):
+        side = pl.ds(pl.multiple_of(q * 512, 512), 512)
+        for move in moves():
+            s = target(move)
+            first = pl.multiple_of(lax.rem(s * group, BLK), group)
+            for n, (src, dst) in enumerate(((e_m, rec_e), (g_m, rec_g))):
+                pltpu.make_async_remote_copy(
+                    src_ref=src.at[(s * group) // BLK, pl.ds(first, group), side],
+                    dst_ref=dst.at[own_place, side],
+                    send_sem=a2a_send,
+                    recv_sem=a2a_recv.at[q, n],
+                    device_id=(s, t),
+                    device_id_type=MESH,
+                ).start()
+
     gather(g_m, g_full, 1, 1)
 
     own_h = (c * group) // BLK
@@ -208,70 +217,33 @@
         pltpu.make_async_copy(diag.at[h], lad_out.at[h, :, at128(t)], own_sem.at[2]).start()
 
     is_owner = lax.rem(t // 2, 2) == core
+    own = 2 * lax.rem(t, 2) + t // 4
+
+    def arrive(full, which):
+        landed = full.at[pl.ds(0, 28 * 16), :]
+        pltpu.make_async_copy(landed, landed, gat_recv.at[which]).wait()
+        for a, b in pairs_of(which):
+            block = full[pl.ds(a * BLK, BLK), pl.ds(b * BLK, BLK)].T
+            full[pl.ds(b * BLK, BLK), pl.ds(a * BLK, BLK)] = block if which else -block
 
     @pl.when(is_owner)
     def _():
-        h = 2 * lax.rem(t, 2) + t // 4
         for j in range(8):
             place = at128(lax.rem(t + j, 8))
             here = pl.ds(j * BLK, BLK)
-            e_full[pl.ds(0, BLK), here] = e_m[h, :, place]
-            g_full[pl.ds(0, BLK), here] = g_m[h, :, place]
-
-        def arrive(full, which):
-            landed = full.at[pl.ds(0, 28 * 16), :]
-            pltpu.make_async_copy(landed, landed, gat_recv.at[which]).wait()
-            for a, b in pairs_of(which):
-                block = full[pl.ds(a * BLK, BLK), pl.ds(b * BLK, BLK)].T
-                full[pl.ds(b * BLK, BLK), pl.ds(a * BLK, BLK)] = block if which else -block
-
+            e_full[pl.ds(0, BLK), here] = e_m[own, :, place]
+            g_full[pl.ds(0, BLK), here] = g_m[own, :, place]
         arrive(e_full, 0)
         for j in range(8):
             here = pl.ds(j * BLK, BLK)
-            weight = wrow[h, :, at128(lax.rem(t + j, 8))].astype(BF)
+            weight = wrow[own, :, at128(lax.rem(t + j, 8))].astype(BF)
             e_full[:, here] = e_full[:, here] * weight
-        arrive(g_full, 1)
-
-        @pl.loop(0, 4)
-        def _(jj):
-            half = pl.ds(pl.multiple_of(jj * 256, 256), 256)
-            total = jnp.dot(e_full[...], g_full[:, half], preferred_element_type=F32)
-            total = total + dot_rows(g_full[...], e_full[half, :])
-            lad_send[:, half] = total.astype(BF)
-            for i in (4, 3, 5, 2, 6, 1, 7):
-                for m in range(2):
-                    j = 2 * jj + m
-
-                    @pl.when(j != i)
-                    def _(i=i, j=j):
-                        pltpu.make_async_remote_copy(
-                            src_ref=lad_send.at[pl.ds(i * BLK, BLK), at128(j)],
-                            dst_ref=lad_out.at[h, :, at128(lax.rem(t + j, 8))],
-                            send_sem=lad_ssem,
-                            recv_sem=lad_rsem,
-                            device_id=(c, lax.rem(t + i, 8)),
-                            device_id_type=MESH,
-                        ).start()
-
-            for m in range(2):
-                j = 2 * jj + m
-
-                @pl.when(j != 0)
-                def _(j=j):
-                    pltpu.make_async_copy(
-                        lad_send.at[pl.ds(0, BLK), at128(j)],
-                        lad_out.at[h, :, at128(lax.rem(t + j, 8))],
-                        own_sem.at[0],
-                    ).start()
-
-    load_w.wait()
-    for n, rec in enumerate((rec_e, rec_g)):
-        landed = rec.at[pl.ds(0, 512 - group), :]
-        pltpu.make_async_copy(landed, landed, a2a_recv.at[n]).wait()
-
-    @pl.loop(0, 2)
-    def _(q):
-        side = pl.ds(pl.multiple_of(q * 512, 512), 512)
+
+    def cross(q):
+        side = pl.ds(q * 512, 512)
+        for n, rec in enumerate((rec_e, rec_g)):
+            landed = rec.at[pl.ds(0, 512 - group), side]
+            pltpu.make_async_copy(landed, landed, a2a_recv.at[q, n]).wait()
         turn = onehot[q]
         scale = wts[q]
         e_bar[...] = (jnp.dot(rec_e[:, side], turn, preferred_element_type=F32) * scale).astype(BF)
@@ -292,6 +264,103 @@
                 device_id_type=MESH,
             ).start()
 
+    load_w.wait()
+    cross(0)
+
+    @pl.when(is_owner)
+    def _():
+        h = own
+        arrive(g_full, 1)
+
+        @pl.loop(0, 4)
+        def _(step):
+            jj = lax.rem(step + 2, 4)
+            half = pl.ds(pl.multiple_of(jj * 256, 256), 256)
+            total = jnp.dot(e_full[...], g_full[:, half], preferred_element_type=F32)
+            total = total + dot_rows(g_full[...], e_full[half, :])
+            lad_send[:, half] = total.astype(BF)
+            for i in (3, 5, 2, 6, 1, 7, 4):
+                for m in range(2):
+                    j = 2 * jj + m
+                    block = lad_send.at[pl.ds(i * BLK, BLK), at128(j)]
+                    to = (c, lax.rem(t + i, 8))
+                    nearer = (1 if i < 4 else 7, 2 if i < 4 else 6)
+                    pass_on = [] if i == 4 else [4] if i in (3, 5) else [4, 3 if i < 4 else 5]
+                    plain = j != i
+                    for k in pass_on:
+                        plain = jnp.logical_and(plain, j != k)
+                    if i in (3, 5):
+                        for k in nearer:
+                            plain = jnp.logical_and(plain, j != k)
+                    if i == 4:
+                        plain = j == 0
+
+                    @pl.when(plain)
+                    def _(j=j, block=block, to=to):
+                        pltpu.make_async_remote_copy(
+                            src_ref=block,
+                            dst_ref=lad_out.at[h, :, at128(lax.rem(t + j, 8))],
+                            send_sem=lad_ssem,
+                            recv_sem=lad_rsem,
+                            device_id=to,
+                            device_id_type=MESH,
+                        ).start()
+
+                    for n, k in enumerate(pass_on):
+
+                        @pl.when(j == k)
+                        def _(n=n, block=block, to=to):
+                            pltpu.make_async_remote_copy(
+                                src_ref=block,
+                                dst_ref=held.at[h, n],
+                                send_sem=lad_ssem,
+                                recv_sem=held_rsem.at[h],
+                                device_id=to,
+                                device_id_type=MESH,
+                            ).start()
+
+            for m in range(2):
+                j = 2 * jj + m
+
+                @pl.when(j != 0)
+                def _(j=j):
+                    pltpu.make_async_copy(
+                        lad_send.at[pl.ds(0, BLK), at128(j)],
+                        lad_out.at[h, :, at128(lax.rem(t + j, 8))],
+                        own_sem.at[0],
+                    ).start()
+
+    cross(1)
+
+    for h in range(4):
+        owner = 4 * (h % 2) + h // 2 + 2 * core
+        delta = lax.rem(t - owner + 8, 8)
+        far = jnp.minimum(delta, 8 - delta)
+        beyond = jnp.where(delta < 4, 3, 5)
+
+        def pass_block(n, place, h=h):
+            turned[h, n] = held[h, n].T
+            pltpu.make_async_copy(held.at[h, n], lad_out.at[h, :, at128(place)], pass_own).start()
+            pltpu.make_async_remote_copy(
+                src_ref=turned.at[h, n],
+                dst_ref=lad_out.at[h, :, at128(t)],
+                send_sem=pass_ssem,
+                recv_sem=lad_rsem,
+                device_id=(c, place),
+                device_id_type=MESH,
+            ).start()
+
+        @pl.when(far == 3)
+        def _(h=h, owner=owner, pass_block=pass_block):
+            pltpu.make_async_copy(held.at[h, 0], held.at[h, 0], held_rsem.at[h]).wait()
+            pass_block(0, lax.rem(owner + 4, 8))
+
+        @pl.when(jnp.logical_or(far == 1, far == 2))
+        def _(h=h, owner=owner, beyond=beyond, pass_block=pass_block):
+            pltpu.make_async_copy(held.at[h], held.at[h], held_rsem.at[h]).wait()
+            pass_block(0, lax.rem(owner + 4, 8))
+            pass_block(1, lax.rem(owner + beyond, 8))
+
     keep = pltpu.make_async_copy(back_send.at[own_place, :], back_out.at[own_place, :], own_sem.at[1])
     keep.start()
 
@@ -305,14 +374,18 @@
     @pl.when(is_owner)
     def _():
         drain(lad_send, 20 * 16, gat_send)
-        drain(lad_send, 49 * 16, lad_ssem)
+        drain(lad_send, 39 * 16, lad_ssem)
+        drain(lad_send, 3 * 16, pass_ssem)
+        drain(lad_send, 3 * 16, pass_own)
         drain(lad_send, 7 * 16, own_sem.at[0])
-        drain(lad_send, 3 * 7 * 16, lad_rsem)
+        drain(lad_send, 18 * 16, lad_rsem)
 
     @pl.when(jnp.logical_not(is_owner))
     def _():
         drain(lad_send, 36 * 16, gat_send)
-        drain(lad_send, 4 * 7 * 16, lad_rsem)
+        drain(lad_send, 21 * 16, lad_rsem)
+        drain(lad_send, 7 * 16, pass_ssem)
+        drain(lad_send, 7 * 16, pass_own)
 
     keep.wait()
     drain(lad_send, 4 * 16, own_sem.at[2])
@@ -352,15 +425,20 @@
             pltpu.VMEM((2, 4, 1024), jnp.int32),
             pltpu.VMEM((2, 2, 512), jnp.int32),
             pltpu.VMEM((2, 512), jnp.int32),
+            pltpu.VMEM((4, 2, BLK, BLK), BF),
+            pltpu.VMEM((4, 2, BLK, BLK), BF),
             dma((5,)),
             dma,
             dma((3,)),
             dma,
+            dma((2, 2)),
+            dma,
             dma((2,)),
             dma,
-            dma((2,)),
-            dma,
-            dma,
+            dma,
+            dma,
+            dma,
+            dma((4,)),
             dma,
             dma,
         ],

time: 56.3 us -> 58.6 us (1.041)
  the two profiles are of different devices: /device:TPU:1 before, /device:TPU:8 now
where the time goes in v4:
time: 58.6 us; the launch traced here: 58.4 us
  Pallas kernels  56.8 us (97%)
  other arithmetic  1.62 us (3%)
    pallas_call x1, Pallas kernels, exchange(): pl.pallas_call(functools.partial(kernel, n_chan), name='commutator_exchan...  56.8 us
    convert_element_type x1, other arithmetic, per_device(): jnp.where((row < sizes) & (column < sizes), total, jnp.zeros((), F32))  1.61 us

profile of v4, /device:TPU:8, one launch (start us, length us, event | category | flops | bytes accessed | tf_op | source)
XLA Modules:
  0.0 58.4 jit_solution(10469765070449089452)
XLA Ops:
  0.0 0.0 copy-start
  0.0 56.8 %commutator_exchange.1 = (bf16[4,128,1024]{2,1,0:T(8,128)(2,1)S(1)}, bf16[512,1024]{1,0:T(8,128)(2,1)S(1)}) custom-call(bf16[4,128,1024]{2,1,0:T(8,128)(2,1)} %e_hbm.1, bf16[4,128,1024]{2,1,0:T(8,128)(2,1)} %g_hbm.1, s32[4]{0:T(128)} %sizes.1, s32[2,4,1024]{2,1,0:T(4,128)} %pocc_hbm.1, s32[2,2,512]{2,1,0:T(2,128)} %rocc_hbm.1, s32[2,512]{1,0:T(2,128)} %cmap_hbm.1, ...), custom_call_target="tpu_custom_call" | custom-call | tf_op jit(solution)/shard_map/commutator_exchange/pallas_call | solution.py:401
  56.8 0.0 copy-done
  56.8 1.6 %fusion.1 = bf16[4,128,1024]{2,1,0:T(8,128)(2,1)} fusion(bf16[4,128,1024]{2,1,0:T(8,128)(2,1)S(1)} %bitcast.2, bf16[4,128,1024]{2,1,0:T(8,128)(2,1)S(1)} %get-tuple-element.7, s32[4]{0:T(128)S(1)} %copy-done, s32[128]{0:T(128)S(1)} %iota_add_fusion), kind=kLoop, calls=%fused_computation.2 | loop fusion | flops 4194304 | bytes 3146256 | tf_op jit(solution)/shard_map/convert_element_type | solution.py:477
  (1 shorter events, 0.0 us)
Async XLA Ops:
  0.0 56.8 %copy-start = (s32[4]{0:T(128)S(1)}, s32[4]{0:T(128)}, u32[]{:S(2)}) copy-start(s32[4]{0:T(128)} %sizes.1) | copy-start | bytes 52

commit v5 on v4

--- a/solution.py
+++ b/solution.py
@@ -44,6 +44,10 @@
             left.remove(taken[-1])
         listed += taken
     return listed[::-1]
+
+
+def passed(i):
+    return {0: (), 4: (), 3: (4,), 5: (4,)}.get(i, (4, 3 if i < 4 else 5))
 
 
 def dot_rows(a, b):
@@ -176,8 +180,9 @@
                     send(j)
 
     gather(e_m, e_full, 0, 0)
+    gather(g_m, g_full, 1, 0)
     gather(e_m, e_full, 0, 1)
-    gather(g_m, g_full, 1, 0)
+    gather(g_m, g_full, 1, 1)
 
     own_place = pl.ds(pl.multiple_of(c * group, group), group)
 
@@ -197,7 +202,6 @@
                     device_id_type=MESH,
                 ).start()
 
-    gather(g_m, g_full, 1, 1)
 
     own_h = (c * group) // BLK
     own_rows = pl.ds(pl.multiple_of(lax.rem(c * group, BLK), group), group)
@@ -264,60 +268,49 @@
                 device_id_type=MESH,
             ).start()
 
-    load_w.wait()
-    cross(0)
-
-    @pl.when(is_owner)
-    def _():
+    def ladder():
         h = own
         arrive(g_full, 1)
 
         @pl.loop(0, 4)
         def _(step):
-            jj = lax.rem(step + 2, 4)
+            jj = lax.rem(6 - step, 4)
             half = pl.ds(pl.multiple_of(jj * 256, 256), 256)
             total = jnp.dot(e_full[...], g_full[:, half], preferred_element_type=F32)
             total = total + dot_rows(g_full[...], e_full[half, :])
             lad_send[:, half] = total.astype(BF)
+
+            def give(i, j, dst, sem):
+                pltpu.make_async_remote_copy(
+                    src_ref=lad_send.at[pl.ds(i * BLK, BLK), at128(j)],
+                    dst_ref=dst,
+                    send_sem=lad_ssem,
+                    recv_sem=sem,
+                    device_id=(c, lax.rem(t + i, 8)),
+                    device_id_type=MESH,
+                ).start()
+
+            for i in (1, 7, 2, 6, 3, 5):
+                for m in range(2):
+                    j = 2 * jj + m
+                    for n, k in enumerate(passed(i)):
+
+                        @pl.when(j == k)
+                        def _(i=i, j=j, n=n):
+                            give(i, j, held.at[h, n], held_rsem.at[h])
+
             for i in (3, 5, 2, 6, 1, 7, 4):
                 for m in range(2):
                     j = 2 * jj + m
-                    block = lad_send.at[pl.ds(i * BLK, BLK), at128(j)]
-                    to = (c, lax.rem(t + i, 8))
-                    nearer = (1 if i < 4 else 7, 2 if i < 4 else 6)
-                    pass_on = [] if i == 4 else [4] if i in (3, 5) else [4, 3 if i < 4 else 5]
-                    plain = j != i
-                    for k in pass_on:
-                        plain = jnp.logical_and(plain, j != k)
-                    if i in (3, 5):
-                        for k in nearer:
+                    plain = j == 0
+                    if i != 4:
+                        plain = j != i
+                        for k in passed(i) + ((1, 2) if i == 3 else (6, 7) if i == 5 else ()):
                             plain = jnp.logical_and(plain, j != k)
-                    if i == 4:
-                        plain = j == 0
 
                     @pl.when(plain)
-                    def _(j=j, block=block, to=to):
-                        pltpu.make_async_remote_copy(
-                            src_ref=block,
-                            dst_ref=lad_out.at[h, :, at128(lax.rem(t + j, 8))],
-                            send_sem=lad_ssem,
-                            recv_sem=lad_rsem,
-                            device_id=to,
-                            device_id_type=MESH,
-                        ).start()
-
-                    for n, k in enumerate(pass_on):
-
-                        @pl.when(j == k)
-                        def _(n=n, block=block, to=to):
-                            pltpu.make_async_remote_copy(
-                                src_ref=block,
-                                dst_ref=held.at[h, n],
-                                send_sem=lad_ssem,
-                                recv_sem=held_rsem.at[h],
-                                device_id=to,
-                                device_id_type=MESH,
-                            ).start()
+                    def _(i=i, j=j):
+                        give(i, j, lad_out.at[h, :, at128(lax.rem(t + j, 8))], lad_rsem)
 
             for m in range(2):
                 j = 2 * jj + m
@@ -329,6 +322,19 @@
                         lad_out.at[h, :, at128(lax.rem(t + j, 8))],
                         own_sem.at[0],
                     ).start()
+
+    late = lax.rem(t, 2) == 1
+
+    @pl.when(jnp.logical_and(is_owner, jnp.logical_not(late)))
+    def _():
+        ladder()
+
+    load_w.wait()
+    cross(0)
+
+    @pl.when(jnp.logical_and(is_owner, late))
+    def _():
+        ladder()
 
     cross(1)
 

time: 58.6 us -> 53.5 us (0.913)
  Pallas kernels: 56.8 us -> 51.8 us
    pallas_call x1, Pallas kernels: 56.8 us -> 51.8 us  [exchange(): pl.pallas_call(functools.partial(kernel, n_chan), name='commutator_exchan...]
where the time goes in v5:
time: 53.5 us
  Pallas kernels  51.8 us (97%)
  other arithmetic  1.62 us (3%)
    pallas_call x1, Pallas kernels, exchange(): pl.pallas_call(functools.partial(kernel, n_chan), name='commutator_exchan...  51.8 us
    convert_element_type x1, other arithmetic, per_device(): jnp.where((row < sizes) & (column < sizes), total, jnp.zeros((), F32))  1.61 us

profile of v5, /device:TPU:8, one launch (start us, length us, event | category | flops | bytes accessed | tf_op | source)
XLA Modules:
  0.0 53.5 jit_solution(12113270288002160268)
XLA Ops:
  0.0 0.0 copy-start
  0.0 51.8 %commutator_exchange.1 = (bf16[4,128,1024]{2,1,0:T(8,128)(2,1)S(1)}, bf16[512,1024]{1,0:T(8,128)(2,1)S(1)}) custom-call(bf16[4,128,1024]{2,1,0:T(8,128)(2,1)} %e_hbm.1, bf16[4,128,1024]{2,1,0:T(8,128)(2,1)} %g_hbm.1, s32[4]{0:T(128)} %sizes.1, s32[2,4,1024]{2,1,0:T(4,128)} %pocc_hbm.1, s32[2,2,512]{2,1,0:T(2,128)} %rocc_hbm.1, s32[2,512]{1,0:T(2,128)} %cmap_hbm.1, ...), custom_call_target="tpu_custom_call" | custom-call | tf_op jit(solution)/shard_map/commutator_exchange/pallas_call | solution.py:407
  51.8 0.0 copy-done
  51.8 1.6 %fusion.1 = bf16[4,128,1024]{2,1,0:T(8,128)(2,1)} fusion(bf16[4,128,1024]{2,1,0:T(8,128)(2,1)S(1)} %bitcast.2, bf16[4,128,1024]{2,1,0:T(8,128)(2,1)S(1)} %get-tuple-element.7, s32[4]{0:T(128)S(1)} %copy-done, s32[128]{0:T(128)S(1)} %iota_add_fusion), kind=kLoop, calls=%fused_computation.2 | loop fusion | flops 4194304 | bytes 3146256 | tf_op jit(solution)/shard_map/convert_element_type | solution.py:483
  (1 shorter events, 0.0 us)
Async XLA Ops:
  0.0 51.8 %copy-start = (s32[4]{0:T(128)S(1)}, s32[4]{0:T(128)}, u32[]{:S(2)}) copy-start(s32[4]{0:T(128)} %sizes.1) | copy-start | bytes 52

commit v6 on v5

--- a/solution.py
+++ b/solution.py
@@ -67,6 +67,7 @@
     rocc_hbm,
     cmap_hbm,
     w_hbm,
+    out,
     lad_out,
     back_out,
     e_m,
@@ -123,7 +124,6 @@
     for load in small:
         load.start()
     load_w = pltpu.make_async_copy(w_hbm, wts, w_sem)
-    load_w.start()
 
     barrier = pltpu.get_barrier_semaphore()
 
@@ -149,6 +149,7 @@
         e_m[h] = e_m[h] * live
         g_m[h] = g_m[h] * live
 
+    load_w.start()
     pl.semaphore_wait(barrier, n_chan + 6)
 
     def gather(src, dst, which, phase):
@@ -310,7 +311,7 @@
 
                     @pl.when(plain)
                     def _(i=i, j=j):
-                        give(i, j, lad_out.at[h, :, at128(lax.rem(t + j, 8))], lad_rsem)
+                        give(i, j, lad_out.at[h, :, at128(lax.rem(t + j, 8))], lad_rsem.at[h])
 
             for m in range(2):
                 j = 2 * jj + m
@@ -323,22 +324,7 @@
                         own_sem.at[0],
                     ).start()
 
-    late = lax.rem(t, 2) == 1
-
-    @pl.when(jnp.logical_and(is_owner, jnp.logical_not(late)))
-    def _():
-        ladder()
-
-    load_w.wait()
-    cross(0)
-
-    @pl.when(jnp.logical_and(is_owner, late))
-    def _():
-        ladder()
-
-    cross(1)
-
-    for h in range(4):
+    def pass_on(h):
         owner = 4 * (h % 2) + h // 2 + 2 * core
         delta = lax.rem(t - owner + 8, 8)
         far = jnp.minimum(delta, 8 - delta)
@@ -351,7 +337,7 @@
                 src_ref=turned.at[h, n],
                 dst_ref=lad_out.at[h, :, at128(t)],
                 send_sem=pass_ssem,
-                recv_sem=lad_rsem,
+                recv_sem=lad_rsem.at[h],
                 device_id=(c, place),
                 device_id_type=MESH,
             ).start()
@@ -366,6 +352,25 @@
             pltpu.make_async_copy(held.at[h], held.at[h], held_rsem.at[h]).wait()
             pass_block(0, lax.rem(owner + 4, 8))
             pass_block(1, lax.rem(owner + beyond, 8))
+
+    late = lax.rem(t, 2) == 1
+
+    @pl.when(jnp.logical_and(is_owner, jnp.logical_not(late)))
+    def _():
+        ladder()
+
+    load_w.wait()
+    cross(0)
+
+    @pl.when(jnp.logical_and(is_owner, late))
+    def _():
+        ladder()
+
+    pass_on(0)
+    pass_on(1)
+    cross(1)
+    pass_on(2)
+    pass_on(3)
 
     keep = pltpu.make_async_copy(back_send.at[own_place, :], back_out.at[own_place, :], own_sem.at[1])
     keep.start()
@@ -384,12 +389,10 @@
         drain(lad_send, 3 * 16, pass_ssem)
         drain(lad_send, 3 * 16, pass_own)
         drain(lad_send, 7 * 16, own_sem.at[0])
-        drain(lad_send, 18 * 16, lad_rsem)
 
     @pl.when(jnp.logical_not(is_owner))
     def _():
         drain(lad_send, 36 * 16, gat_send)
-        drain(lad_send, 21 * 16, lad_rsem)
         drain(lad_send, 7 * 16, pass_ssem)
         drain(lad_send, 7 * 16, pass_own)
 
@@ -398,22 +401,41 @@
     drain(rec_e, 512 - group, back_ssem)
     drain(rec_e, 512 - group, back_rsem)
 
+    for h in range(4):
+        delta = lax.rem(t - (4 * (h % 2) + h // 2 + 2 * core) + 8, 8)
+        far = jnp.minimum(delta, 8 - delta)
+
+        @pl.when(jnp.logical_or(far == 1, far == 2))
+        def _(h=h):
+            drain(lad_send, 5 * 16, lad_rsem.at[h])
+
+        @pl.when(far == 3)
+        def _(h=h):
+            drain(lad_send, 6 * 16, lad_rsem.at[h])
+
+        @pl.when(far == 4)
+        def _(h=h):
+            drain(lad_send, 7 * 16, lad_rsem.at[h])
+
+        size = sizes[h]
+        live = (rows < size).astype(F32) * (cols < size).astype(F32)
+        total = lad_out[h].astype(F32) + back_out[pl.ds(h * BLK, BLK), :].astype(F32)
+        out[h] = jnp.where(live > 0, total, 0.0).astype(BF)
+
 
 def exchange(n_chan, *args):
     far = pl.BlockSpec(memory_space=pltpu.HBM)
     smem = pl.BlockSpec(memory_space=pltpu.SMEM)
-    anywhere = pl.BlockSpec(memory_space=pl.ANY)
     dma = pltpu.SemaphoreType.DMA
     return pl.pallas_call(
         functools.partial(kernel, n_chan),
         name="commutator_exchange",
-        out_shape=(
-            jax.ShapeDtypeStruct((4, BLK, 1024), BF),
-            jax.ShapeDtypeStruct((512, 1024), BF),
-        ),
+        out_shape=jax.ShapeDtypeStruct((4, BLK, 1024), BF),
         in_specs=[far, far, smem, far, far, far, far],
-        out_specs=(anywhere, anywhere),
+        out_specs=pl.BlockSpec(memory_space=pltpu.VMEM),
         scratch_shapes=[
+            pltpu.VMEM((4, BLK, 1024), BF),
+            pltpu.VMEM((512, 1024), BF),
             pltpu.VMEM((4, BLK, 1024), BF),
             pltpu.VMEM((4, BLK, 1024), BF),
             pltpu.VMEM((512, 1024), BF),
@@ -441,7 +463,7 @@
             dma,
             dma((2,)),
             dma,
-            dma,
+            dma((4,)),
             dma,
             dma,
             dma((4,)),
@@ -464,8 +486,7 @@
     recouple_map,
     recouple_weights,
 ):
-    chan_count, tile_rows, states = generator.shape
-    ladder, back = exchange(
+    return exchange(
         n_chan,
         generator,
         hamiltonian,
@@ -475,12 +496,6 @@
         recouple_map,
         recouple_weights,
     )
-    shape = (chan_count, tile_rows, states)
-    sizes = chan_sizes[:, None, None]
-    row = lax.axis_index("tile") * tile_rows + lax.broadcasted_iota(jnp.int32, shape, 1)
-    column = lax.broadcasted_iota(jnp.int32, shape, 2)
-    total = ladder.astype(F32) + back.reshape(shape).astype(F32)
-    return jnp.where((row < sizes) & (column < sizes), total, jnp.zeros((), F32)).astype(BF)
 
 
 def solution(mesh):

time: 53.5 us -> 53 us (level)
  other arithmetic: 1.62 us -> 0 us
  local copies, waits for them, and re-layouts: 0.01 us -> 0.97 us
    convert_element_type x1 -> x0, other arithmetic: 1.61 us -> none  [per_device(): jnp.where((row < sizes) & (column < sizes), total, jnp.zeros((), F32))]
    unnamed x2 -> x1, local copies, waits for them, and re-layouts: 0.01 us -> 0.97 us
where the time goes in v6:
time: 53 us; the launch traced here: 52.8 us
  Pallas kernels  51.9 us (98%)
  local copies, waits for them, and re-layouts  0.97 us (2%)
    pallas_call x1, Pallas kernels, exchange(): pl.pallas_call(functools.partial(kernel, n_chan), name='commutator_exchan...  51.9 us

profile of v6, /device:TPU:8, one launch (start us, length us, event | category | flops | bytes accessed | tf_op | source)
XLA Modules:
  0.0 52.8 jit_solution(9302803298629354891)
XLA Ops:
  0.0 51.9 %commutator_exchange.1 = bf16[4,128,1024]{2,1,0:T(8,128)(2,1)S(1)} custom-call(bf16[4,128,1024]{2,1,0:T(8,128)(2,1)} %e_hbm.1, bf16[4,128,1024]{2,1,0:T(8,128)(2,1)} %g_hbm.1, s32[4]{0:T(128)} %sizes.1, s32[2,4,1024]{2,1,0:T(4,128)} %pocc_hbm.1, s32[2,2,512]{2,1,0:T(2,128)} %rocc_hbm.1, s32[2,512]{1,0:T(2,128)} %cmap_hbm.1, f32[2,512,512]{2,1,0:T(8,128)} %w_hbm.1), custom_call_target="tpu_custom_call" | custom-call | tf_op jit(solution)/shard_map/commutator_exchange/pallas_call | solution.py:430
  51.9 1.0 %copy.9 = bf16[4,128,1024]{2,1,0:T(8,128)(2,1)} copy(bf16[4,128,1024]{2,1,0:T(8,128)(2,1)S(1)} %commutator_exchange.1) | data formatting | bytes 2097152

commit v7 on v6

--- a/solution.py
+++ b/solution.py
@@ -379,26 +379,17 @@
         piece = ref.at[pl.ds(0, count), :]
         pltpu.make_async_copy(piece, piece, sem).wait()
 
-    for n in range(2):
-        drain(rec_e, 512 - group, a2a_send)
-
     @pl.when(is_owner)
     def _():
-        drain(lad_send, 20 * 16, gat_send)
-        drain(lad_send, 39 * 16, lad_ssem)
-        drain(lad_send, 3 * 16, pass_ssem)
         drain(lad_send, 3 * 16, pass_own)
         drain(lad_send, 7 * 16, own_sem.at[0])
 
     @pl.when(jnp.logical_not(is_owner))
     def _():
-        drain(lad_send, 36 * 16, gat_send)
-        drain(lad_send, 7 * 16, pass_ssem)
         drain(lad_send, 7 * 16, pass_own)
 
     keep.wait()
     drain(lad_send, 4 * 16, own_sem.at[2])
-    drain(rec_e, 512 - group, back_ssem)
     drain(rec_e, 512 - group, back_rsem)
 
     for h in range(4):
@@ -421,6 +412,22 @@
         live = (rows < size).astype(F32) * (cols < size).astype(F32)
         total = lad_out[h].astype(F32) + back_out[pl.ds(h * BLK, BLK), :].astype(F32)
         out[h] = jnp.where(live > 0, total, 0.0).astype(BF)
+
+    for n in range(2):
+        drain(rec_e, 512 - group, a2a_send)
+
+    @pl.when(is_owner)
+    def _():
+        drain(lad_send, 20 * 16, gat_send)
+        drain(lad_send, 39 * 16, lad_ssem)
+        drain(lad_send, 3 * 16, pass_ssem)
+
+    @pl.when(jnp.logical_not(is_owner))
+    def _():
+        drain(lad_send, 36 * 16, gat_send)
+        drain(lad_send, 7 * 16, pass_ssem)
+
+    drain(rec_e, 512 - group, back_ssem)
 
 
 def exchange(n_chan, *args):

time: 53 us -> 53 us (level)
  no operation moved by 1% of the time
where the time goes in v7:
time: 53 us; the launch traced here: 52.9 us
  Pallas kernels  51.9 us (98%)
  local copies, waits for them, and re-layouts  0.97 us (2%)
    pallas_call x1, Pallas kernels, exchange(): pl.pallas_call(functools.partial(kernel, n_chan), name='commutator_exchan...  51.9 us

profile of v7, /device:TPU:8, one launch (start us, length us, event | category | flops | bytes accessed | tf_op | source)
XLA Modules:
  0.0 52.9 jit_solution(1493653814973961639)
XLA Ops:
  0.0 51.9 %commutator_exchange.1 = bf16[4,128,1024]{2,1,0:T(8,128)(2,1)S(1)} custom-call(bf16[4,128,1024]{2,1,0:T(8,128)(2,1)} %e_hbm.1, bf16[4,128,1024]{2,1,0:T(8,128)(2,1)} %g_hbm.1, s32[4]{0:T(128)} %sizes.1, s32[2,4,1024]{2,1,0:T(4,128)} %pocc_hbm.1, s32[2,2,512]{2,1,0:T(2,128)} %rocc_hbm.1, s32[2,512]{1,0:T(2,128)} %cmap_hbm.1, f32[2,512,512]{2,1,0:T(8,128)} %w_hbm.1), custom_call_target="tpu_custom_call" | custom-call | tf_op jit(solution)/shard_map/commutator_exchange/pallas_call | solution.py:437
  51.9 1.0 %copy.9 = bf16[4,128,1024]{2,1,0:T(8,128)(2,1)} copy(bf16[4,128,1024]{2,1,0:T(8,128)(2,1)S(1)} %commutator_exchange.1) | data formatting | bytes 2097152

commit v8 on v6

--- a/solution.py
+++ b/solution.py
@@ -273,10 +273,8 @@
         h = own
         arrive(g_full, 1)
 
-        @pl.loop(0, 4)
-        def _(step):
-            jj = lax.rem(6 - step, 4)
-            half = pl.ds(pl.multiple_of(jj * 256, 256), 256)
+        for jj in (2, 1, 0, 3):
+            half = pl.ds(jj * 256, 256)
             total = jnp.dot(e_full[...], g_full[:, half], preferred_element_type=F32)
             total = total + dot_rows(g_full[...], e_full[half, :])
             lad_send[:, half] = total.astype(BF)
@@ -295,9 +293,7 @@
                 for m in range(2):
                     j = 2 * jj + m
                     for n, k in enumerate(passed(i)):
-
-                        @pl.when(j == k)
-                        def _(i=i, j=j, n=n):
+                        if j == k:
                             give(i, j, held.at[h, n], held_rsem.at[h])
 
             for i in (3, 5, 2, 6, 1, 7, 4):
@@ -307,17 +303,14 @@
                     if i != 4:
                         plain = j != i
                         for k in passed(i) + ((1, 2) if i == 3 else (6, 7) if i == 5 else ()):
-                            plain = jnp.logical_and(plain, j != k)
-
-                    @pl.when(plain)
-                    def _(i=i, j=j):
+                            plain = plain and j != k
+
+                    if plain:
                         give(i, j, lad_out.at[h, :, at128(lax.rem(t + j, 8))], lad_rsem.at[h])
 
             for m in range(2):
                 j = 2 * jj + m
-
-                @pl.when(j != 0)
-                def _(j=j):
+                if j != 0:
                     pltpu.make_async_copy(
                         lad_send.at[pl.ds(0, BLK), at128(j)],
                         lad_out.at[h, :, at128(lax.rem(t + j, 8))],

time: 53 us -> 54.8 us (1.034)
  the two profiles are of different devices: /device:TPU:8 before, /device:TPU:32 now
where the time goes in v8:
time: 54.8 us; the launch traced here: 54.7 us
  Pallas kernels  53.7 us (98%)
  local copies, waits for them, and re-layouts  0.97 us (2%)
    pallas_call x1, Pallas kernels, exchange(): pl.pallas_call(functools.partial(kernel, n_chan), name='commutator_exchan...  53.7 us

profile of v8, /device:TPU:32, one launch (start us, length us, event | category | flops | bytes accessed | tf_op | source)
XLA Modules:
  0.0 54.7 jit_solution(6854273333213933004)
XLA Ops:
  0.0 53.7 %commutator_exchange.1 = bf16[4,128,1024]{2,1,0:T(8,128)(2,1)S(1)} custom-call(bf16[4,128,1024]{2,1,0:T(8,128)(2,1)} %e_hbm.1, bf16[4,128,1024]{2,1,0:T(8,128)(2,1)} %g_hbm.1, s32[4]{0:T(128)} %sizes.1, s32[2,4,1024]{2,1,0:T(4,128)} %pocc_hbm.1, s32[2,2,512]{2,1,0:T(2,128)} %rocc_hbm.1, s32[2,512]{1,0:T(2,128)} %cmap_hbm.1, f32[2,512,512]{2,1,0:T(8,128)} %w_hbm.1), custom_call_target="tpu_custom_call" | custom-call | tf_op jit(solution)/shard_map/commutator_exchange/pallas_call | solution.py:423
  53.7 1.0 %copy.9 = bf16[4,128,1024]{2,1,0:T(8,128)(2,1)} copy(bf16[4,128,1024]{2,1,0:T(8,128)(2,1)S(1)} %commutator_exchange.1) | data formatting | bytes 2097152
